TPU v7x, 32 devices: a whole 2x2x4 slice. The times are simulated.
32 devices in a mesh: ctx: 8 (over z, x), head: 4 (over y, core).
Axes of the slice: x: 2, y: 2, z: 4, core: 2. Of those that a mesh axis runs over, the one named last changes fastest.
Arguments:
- probe_vectors: bfloat16 [1024, 8192], P('ctx', 'head'), may hold values from -160 to 160
- lookup_tensor: bfloat16 [8192, 1024], P('ctx', 'head'), may hold values from -4.5 to 4.5
- payload_tensor: bfloat16 [8192, 1024], P('ctx', 'head'), may hold values from -6 to 6
- sequence_locations: int32 [1024], replicated, may hold values from 0 to 8191, as said below
- attention_return_matrix: bfloat16 [8192, 8192], P('head', 'ctx'), may hold values from -0.0625 to 0.0625
- skip_stream_state: bfloat16 [1024, 8192], P('head', 'ctx'), may hold values from -4 to 4
- early_rescaling_factor: float32 [8192], P('ctx'), may hold values from 0.5 to 1.5
- lexicon_projection_matrix: bfloat16 [8192, 65536], P(None, ('ctx', 'head')), may hold values from -0.1875 to 0.1875
- calibrating_divisor: float32 [1024], replicated, may hold values from 0.02 to 1
- desired_tokens_list: int32 [1024], replicated, may hold values from 0 to 65535
Outputs:
- hidden: bfloat16 [1024, 8192], P('head', 'ctx')
- logprob: float32 [1024], replicated
Inputs may be any that keep to these rules, and one draw needn't show every extreme that they name: `sequence_locations`: query i stands at a position from i * 8 to (i + 1) * 8 - 1; the last query stands at 8191.
All inputs are finite; a program needn't handle non-finite values.
Results may differ from a plain program's by a relative error of at most 0.0014.
The roundings to bfloat16 on the way count: a program that leaves them out, or rounds other values in their place, can miss the bound.
Values may be sent and summed in bfloat16 or wider, within the bound.
No kernel may reach another device: no remote copies, remote signals or barrier semaphores. Data moves between devices by JAX's collectives and lax.ppermute only.
A program may use at most 192 MiB of HBM per device.

v0:
```python
import functools
import math

import jax
import jax.numpy as jnp
import numpy as np
from jax import lax
from jax.experimental import pallas as pl
from jax.experimental.pallas import tpu as pltpu
from jax.sharding import PartitionSpec as P

HEAD_SIZE = 128

neg_big = -1e30
eps = 1e-05
AXES = ("ctx", "head")


class Moves:
    def __init__(self, mesh):
        self.ctx, self.head = mesh.shape["ctx"], mesh.shape["head"]

    def perm(self, ctx_to=None, head_to=None):
        pairs = []
        for i in range(self.ctx):
            for h in range(self.head):
                i2 = i if ctx_to is None else ctx_to(i)
                h2 = h if head_to is None else head_to(h)
                if i2 is not None and h2 is not None:
                    pairs.append((i * self.head + h, i2 * self.head + h2))
        return pairs

    def ctx_move(self, value, ctx_to):
        return lax.ppermute(value, AXES, self.perm(ctx_to=ctx_to))

    def head_move(self, value, head_to):
        return lax.ppermute(value, AXES, self.perm(head_to=head_to))

    def minor_swap(self, value):
        return self.ctx_move(value, lambda i: i ^ 1)

    def y_swap(self, value):
        return self.head_move(value, lambda h: h ^ 2)

    def core_swap(self, value):
        return self.head_move(value, lambda h: h ^ 1)


def ring_order(count):
    return list(range(0, count, 2)) + list(range(count - 1, 0, -2))


def ring_gather(moves, block, count, ahead, behind, halves=False):
    order = ring_order(count)
    place = {v: p for p, v in enumerate(order)}

    def shifted(i, step):
        base = i // count * count
        return base + order[(place[i - base] + step) % count]

    def source(step):
        return np.array([shifted(i, step) for i in range(moves.ctx)], np.int32)

    def forward_move(value):
        return moves.ctx_move(value, lambda i: shifted(i, 1))

    def backward_move(value):
        return moves.ctx_move(value, lambda i: shifted(i, -1))

    found = [(source(0), block)]
    forward = backward = block
    for k in range(1, max(ahead, behind) + 1):
        if k <= ahead:
            forward = forward_move(forward)
            found.append((source(-k), forward))
        if k <= behind:
            backward = backward_move(backward)
            found.append((source(k), backward))
    if halves:
        cut, k = block.shape[0] // 2, ahead + 1
        last = [forward_move(forward[:cut]), backward_move(backward[cut:])]
        found.append((source(k), jnp.concatenate(last)))
    return found


def square_gather(moves, kept, came):
    def origin(step):
        return np.arange(moves.ctx, dtype=np.int32) ^ step

    def move(value, step):
        return moves.ctx_move(value, lambda i: i ^ step)

    kept_z = move(kept, 2)
    kept_x = move(kept, 1)
    kept_xz = move(kept_z, 1)
    came_x = move(came, 1)
    came_z = move(came, 2)
    far = jnp.stack([move(came_x[0], 2), move(came_z[1], 1)])
    return (
        [(origin(0), kept), (origin(1), kept_x), (origin(2), kept_z), (origin(3), kept_xz)],
        [(origin(0), came), (origin(1), came_x), (origin(2), came_z), (origin(3), far)],
    )


def line_slots(length):
    arrivals = []
    for z in range(length):
        mine = []
        for k in range(1, length):
            pair = []
            if z + k < length:
                pair.append(("down", k, z + k))
            if z - k >= 0:
                pair.append(("up", k, z - k))
            if z >= length // 2:
                pair.reverse()
            mine += pair
        arrivals.append(mine)
    return [[arrivals[z][s] for z in range(length)] for s in range(length - 1)]


def line_gather(moves, block, z, arrived):
    length = moves.ctx // 2
    got = {("up", 0): block, ("down", 0): block}
    slots = line_slots(length)
    value, gate = block, arrived(0, block)
    for k in range(1, length):
        got["up", k] = moves.ctx_move(
            got["up", k - 1], lambda i: i + 2 if k - 1 <= i // 2 < length - 1 else None
        )
        got["down", k] = moves.ctx_move(
            got["down", k - 1], lambda i: i - 2 if 0 < i // 2 <= length - k else None
        )
        slot = slots[k - 1]
        choices = {}
        for place, (way, r, _) in enumerate(slot):
            choices.setdefault((way, r), []).append(place)
        options, *_ = lax.optimization_barrier(([got[key] for key in choices], value, gate))
        value = options[0]
        for option, where_z in list(zip(options, choices.values()))[1:]:
            here = functools.reduce(jnp.logical_or, [z == p for p in where_z])
            value = jnp.where(here, option, value)
        gate = arrived(k, value)


def ctx_butterfly(moves, value, merge):
    step = 1
    while step < moves.ctx:
        came = moves.ctx_move(value, lambda i: i ^ step)
        value = merge(value, came)
        step *= 2
    return value


def butterfly(moves, value, merge):
    step = 1
    while step < moves.head:
        value = merge(value, moves.head_move(value, lambda h: h ^ step))
        step *= 2
    return ctx_butterfly(moves, value, merge)


def attention_kernel(count, heads, table, loc_ref, q_ref, *rest):
    sources, (o_ref, k_buf, v_buf, sems) = rest[:count], rest[count:]
    block = pl.program_id(0)
    span = k_buf.shape[1]
    rows = q_ref.shape[1]
    factor = HEAD_SIZE ** (-0.5) * math.log2(math.e)

    @pl.when(block == 0)
    def _():
        copies = []
        for n, source in enumerate(sources):
            for part, buf in enumerate((k_buf, v_buf)):
                copies.append(
                    pltpu.make_async_copy(source.at[part], buf.at[table[n]], sems.at[n, part])
                )
        for copy in copies:
            copy.start()
        for copy in copies:
            copy.wait()

    query = jnp.concatenate(
        [q_ref[0, :, n * HEAD_SIZE : (n + 1) * HEAD_SIZE] for n in range(heads)], axis=0
    )

    def attend(j, carry, masked):
        run_max, run_sum, run_acc = carry
        scores = lax.dot_general(
            query, k_buf[j], (((1,), (1,)), ((), ())), preferred_element_type=jnp.float32
        )
        if masked:
            row_pos = jnp.concatenate([loc_ref[0]] * heads, axis=0)
            key_pos = j * span + lax.broadcasted_iota(jnp.int32, scores.shape, 1)
            scores = jnp.where(key_pos <= row_pos, scores, neg_big)
        block_max = jnp.max(scores, axis=1, keepdims=True)
        weights = jnp.exp2((scores - block_max) * factor)
        block_sum = jnp.sum(weights, axis=1, keepdims=True)
        block_acc = jnp.dot(
            weights.astype(jnp.bfloat16), v_buf[j], preferred_element_type=jnp.float32
        )
        new_max = jnp.maximum(run_max, block_max)
        old = jnp.exp2((run_max - new_max) * factor)
        new = jnp.exp2((block_max - new_max) * factor)
        return new_max, run_sum * old + block_sum * new, run_acc * old + block_acc * new

    start = (
        jnp.full((rows * heads, 1), neg_big, jnp.float32),
        jnp.zeros((rows * heads, 1), jnp.float32),
        jnp.zeros((rows * heads, HEAD_SIZE), jnp.float32),
    )
    carry = lax.fori_loop(0, block, lambda j, c: attend(j, c, False), start)
    _, total, acc = attend(block, carry, True)
    out = (acc / total).astype(o_ref.dtype)
    for n in range(heads):
        o_ref[0, :, n * HEAD_SIZE : (n + 1) * HEAD_SIZE] = out[n * rows : (n + 1) * rows]


def attention(query, locations, blocks, table):
    row_blocks, rows, width = query.shape
    count, span = len(blocks), blocks[0].shape[1]
    heads = width // HEAD_SIZE
    pairs = row_blocks * (row_blocks + 1) // 2 * rows * heads * span
    return pl.pallas_call(
        functools.partial(attention_kernel, count, heads),
        out_shape=jax.ShapeDtypeStruct(query.shape, jnp.bfloat16),
        grid_spec=pltpu.PrefetchScalarGridSpec(
            num_scalar_prefetch=1,
            grid=(row_blocks,),
            in_specs=[
                pl.BlockSpec((1, rows, 1), lambda b, t: (b, 0, 0)),
                pl.BlockSpec((1, rows, width), lambda b, t: (b, 0, 0)),
            ]
            + [pl.BlockSpec(memory_space=pl.ANY)] * count,
            out_specs=pl.BlockSpec((1, rows, width), lambda b, t: (b, 0, 0)),
            scratch_shapes=[
                pltpu.VMEM((count, span, HEAD_SIZE), jnp.bfloat16),
                pltpu.VMEM((count, span, HEAD_SIZE), jnp.bfloat16),
                pltpu.SemaphoreType.DMA((count, 2)),
            ],
        ),
        compiler_params=pltpu.CompilerParams(
            dimension_semantics=("arbitrary",), vmem_limit_bytes=40 << 20
        ),
        cost_estimate=pl.CostEstimate(
            flops=4 * pairs * HEAD_SIZE,
            bytes_accessed=4 * count * span * HEAD_SIZE + 4 * query.size,
            transcendentals=pairs,
        ),
    )(table, locations, query, *blocks)


def project_kernel(count, has_before, info, *refs):
    refs = list(refs)
    before = refs.pop(0) if has_before else None
    out = refs.pop()
    total = before[...] if has_before else None
    for n in range(count):
        term = jnp.dot(refs[n][...], refs[count + n][...], preferred_element_type=jnp.float32)
        total = term if total is None else total + term
    out[...] = total


def project(info, blocks, matrix, before, start, tiles, rows):
    count, depth = len(blocks), blocks[0].shape[1]
    width = matrix.shape[1]
    row_tile = pl.BlockSpec((rows, depth), lambda r, i: (i[start + r], 0))
    in_specs = [row_tile] * count
    for n in range(count):
        in_specs.append(pl.BlockSpec((depth, width), lambda r, i, n=n: (i[n], 0)))
    args = [*blocks] + [matrix] * count
    if before is not None:
        in_specs.insert(0, pl.BlockSpec((rows, width), lambda r, i: (i[start + r], 0)))
        args.insert(0, before)
    return pl.pallas_call(
        functools.partial(project_kernel, count, before is not None),
        out_shape=jax.ShapeDtypeStruct((tiles * rows, width), jnp.float32),
        grid_spec=pltpu.PrefetchScalarGridSpec(
            num_scalar_prefetch=1,
            grid=(tiles,),
            in_specs=in_specs,
            out_specs=pl.BlockSpec((rows, width), lambda r, i: (r, 0)),
        ),
        compiler_params=pltpu.CompilerParams(
            dimension_semantics=("arbitrary",), vmem_limit_bytes=40 << 20
        ),
        cost_estimate=pl.CostEstimate(
            flops=2 * tiles * rows * count * depth * width,
            bytes_accessed=2 * count * depth * (width + tiles * rows) + 4 * tiles * rows * width,
            transcendentals=0,
        ),
    )(info, *args)


def normalize_kernel(scale_ref, far_ref, gain_ref, *refs):
    parts, out_ref = refs[:-1], refs[-1]
    rows = parts[0].shape[0]
    for n, part in enumerate(parts):
        by = (scale_ref, far_ref)[n % 2][...]
        wide = part[...].astype(jnp.float32) * by * gain_ref[n // 2]
        out_ref[n // 2, n % 2 * rows : (n % 2 + 1) * rows] = wide.astype(out_ref.dtype)


def normalize(parts, scale, far_scale, gain):
    rows, depth = parts[0].shape
    return pl.pallas_call(
        normalize_kernel,
        out_shape=jax.ShapeDtypeStruct((2, 2 * rows, depth), jnp.bfloat16),
        compiler_params=pltpu.CompilerParams(vmem_limit_bytes=12 << 20),
        cost_estimate=pl.CostEstimate(
            flops=8 * rows * depth, bytes_accessed=16 * rows * depth, transcendentals=0
        ),
    )(scale, far_scale, gain[:, None, :], *parts)


def exit_kernel(final, has_before, info, own_ref, other_ref, *rest):
    rest = list(rest)
    steps, rows = own_ref.shape[:2]
    lex_refs, rest = rest[:steps], rest[steps:]
    before = rest.pop(0) if has_before else None
    part_width = lex_refs[0].shape[1] // 2
    tile, tiles = pl.program_id(0), pl.num_programs(0)

    def product(n, part):
        columns = slice(part * part_width, (part + 1) * part_width)
        total = before[n * rows : (n + 1) * rows, columns] if has_before else None
        ref = (own_ref, other_ref)[n]
        for k in range(steps):
            term = jnp.dot(ref[k], lex_refs[k][:, columns], preferred_element_type=jnp.float32)
            total = term if total is None else total + term
        return total

    if not final:
        (out_ref,) = rest
        for part in range(2):
            for n in range(2):
                out_ref[
                    n * rows : (n + 1) * rows, part * part_width : (part + 1) * part_width
                ] = product(n, part)
        return

    div_ref, token_ref, out_ref, first, second, tops, weights, picks = rest
    group = div_ref.shape[1]
    groups = 2 * rows // group
    inverse = [1.0 / div_ref[info[steps + g]] for g in range(groups)]

    @pl.when(tile == 0)
    def _():
        second[...] = jnp.full(second.shape, neg_big, jnp.float32)
        tops[...] = jnp.full(tops.shape, neg_big, jnp.float32)
        weights[...] = jnp.zeros(weights.shape, jnp.float32)
        picks[...] = jnp.zeros(picks.shape, jnp.float32)

    def count_in(ref, start, valid):
        for g in range(groups):
            part = slice(g * group, (g + 1) * group)
            value = ref[part]
            factor = inverse[g] * math.log2(math.e)
            token = token_ref[info[steps + g]] - start
            token = jnp.where(valid, token, -1)
            column = lax.broadcasted_iota(jnp.int32, value.shape, 1)
            found = jnp.sum(jnp.where(column == token, value, 0.0), axis=1, keepdims=True)
            top = tops[part]
            new_top = jnp.maximum(top, jnp.max(value, axis=1, keepdims=True))
            fresh = jnp.sum(jnp.exp2((value - new_top) * factor), axis=1, keepdims=True)
            weights[part] = weights[part] * jnp.exp2((top - new_top) * factor) + fresh
            tops[part] = new_top
            picks[part] += found

    start = info[steps + groups] + 2 * tile * part_width
    count_in(second, start - part_width, tile > 0)
    for n in range(2):
        first[n * rows : (n + 1) * rows] = product(n, 0)
    count_in(first, start, True)
    for n in range(2):
        second[n * rows : (n + 1) * rows] = product(n, 1)

    @pl.when(tile == tiles - 1)
    def _():
        count_in(second, start + part_width, True)
        for g in range(groups):
            part = slice(g * group, (g + 1) * group)
            lane = lax.broadcasted_iota(jnp.int32, (group, out_ref.shape[1]), 1)
            out_ref[part] = jnp.where(
                lane == 0,
                tops[part] * inverse[g],
                jnp.where(lane == 1, weights[part], picks[part] * inverse[g]),
            )


def exit_piece(info, own, other, lexicon, before, row_args):
    steps, rows, depth = own.shape
    width = lexicon.shape[1]
    tile = min(512, width)
    final = row_args is not None
    once = lambda a: pl.BlockSpec(
        a.shape, lambda n, i: (0,) * a.ndim, pipeline_mode=pl.Buffered(1)
    )
    wide = pl.BlockSpec((2 * rows, tile), lambda n, i: (0, n))
    in_specs = [once(own), once(other)]
    args = [info, own, other] + [lexicon] * steps
    for k in range(steps):
        in_specs.append(pl.BlockSpec((depth, tile), lambda n, i, k=k: (i[k], n)))
    if before is not None:
        in_specs.append(wide)
        args.append(pltpu.with_memory_space_constraint(before, pltpu.HBM))
    if final:
        in_specs += [once(a) for a in row_args]
        args += list(row_args)
        out_shape = jax.ShapeDtypeStruct((2 * rows, 128), jnp.float32)
        out_specs = pl.BlockSpec((2 * rows, 128), lambda n, i: (0, 0))
        scratch = [pltpu.VMEM((2 * rows, tile // 2), jnp.float32)] * 2
        scratch += [pltpu.VMEM((2 * rows, 1), jnp.float32)] * 3
    else:
        out_shape = pltpu.HBM((2 * rows, width), jnp.float32)
        out_specs = wide
        scratch = []
    return pl.pallas_call(
        functools.partial(exit_kernel, final, before is not None),
        out_shape=out_shape,
        grid_spec=pltpu.PrefetchScalarGridSpec(
            num_scalar_prefetch=1,
            grid=(width // tile,),
            in_specs=in_specs,
            out_specs=out_specs,
            scratch_shapes=scratch,
        ),
        compiler_params=pltpu.CompilerParams(
            dimension_semantics=("arbitrary",), vmem_limit_bytes=32 << 20
        ),
        cost_estimate=pl.CostEstimate(
            flops=4 * steps * rows * depth * width,
            bytes_accessed=2 * steps * depth * (width + 2 * rows),
            transcendentals=0,
        ),
    )(*args)


def shards(
    moves,
    probe_vectors,
    lookup_tensor,
    payload_tensor,
    sequence_locations,
    attention_return_matrix,
    skip_stream_state,
    early_rescaling_factor,
    lexicon_projection_matrix,
    calibrating_divisor,
    desired_tokens_list,
):
    return body(
        moves,
        probe_vectors,
        lookup_tensor,
        payload_tensor,
        sequence_locations,
        attention_return_matrix,
        skip_stream_state,
        early_rescaling_factor,
        lexicon_projection_matrix,
        calibrating_divisor,
        desired_tokens_list,
    )


def body(
    moves,
    probe_vectors,
    lookup_tensor,
    payload_tensor,
    sequence_locations,
    attention_return_matrix,
    skip_stream_state,
    early_rescaling_factor,
    lexicon_projection_matrix,
    calibrating_divisor,
    desired_tokens_list,
):
    ctx, head = moves.ctx, moves.head
    i, h = lax.axis_index("ctx"), lax.axis_index("head")
    rows_here, width_here = probe_vectors.shape
    heads_here = width_here // HEAD_SIZE
    total_rows = rows_here * ctx
    kv_here = lookup_tensor.shape[1] // HEAD_SIZE
    half = ctx // kv_here
    head_parts = min(ctx, heads_here)
    row_parts = ctx // head_parts
    part_rows, part_width = rows_here // row_parts, width_here // head_parts

    mine = i // half

    def of_head(which):
        start = which * HEAD_SIZE
        return jnp.stack(
            [
                lax.dynamic_slice_in_dim(a, start, HEAD_SIZE, 1)
                for a in (lookup_tensor, payload_tensor)
            ]
        )

    kept = [(np.arange(ctx, dtype=np.int32), of_head(mine))]
    for shift in range(1, kv_here):
        sent = of_head((mine + shift) % kv_here)
        came = moves.ctx_move(sent, lambda s: (s + shift * half) % ctx)
        kept.append((np.array([(s - shift * half) % ctx for s in range(ctx)], np.int32), came))
    blocks, tables = [], []
    squares = square_gather(moves, kept[0][1], kept[1][1]) if (half, kv_here) == (4, 2) else None
    for n, (origin, block) in enumerate(kept):
        if squares is not None:
            blocks += [got for _, got in squares[n]]
            tables += [origin[source] for source, _ in squares[n]]
            continue
        long, short = half // 2, half - 1 - half // 2
        ahead, behind = (long, short) if n % 2 == 0 else (short, long)
        for source, got in ring_gather(moves, block, half, ahead, behind):
            blocks.append(got)
            tables.append(origin[source])
    table = jnp.asarray(np.stack(tables, 1))[i]

    gain = early_rescaling_factor[None]
    step = 1
    while step < ctx:
        came = moves.ctx_move(gain, lambda n: n ^ step)
        gain = jnp.concatenate([gain, came])
        step *= 2
    slots = [[(None, 0, z) for z in range(ctx // 2)]] + line_slots(ctx // 2)
    vocab_here = lexicon_projection_matrix.shape[1]
    infos = np.zeros((ctx, head, len(slots), 7), np.int32)
    for a, b in np.ndindex(ctx, head):
        for n, slot in enumerate(slots):
            place = slot[a // 2][2] * 2
            infos[a, b, n, :2] = place + a % 2, place + 1 - a % 2
            infos[a, b, n, 2:] = b, b ^ 2, b ^ 1, b ^ 3, (a * head + b) * vocab_here
    infos = jnp.asarray(infos)[i, h]
    gains = jnp.take(gain, infos[:, :2] ^ i, axis=0, mode="clip")
    infos = [infos[n] for n in range(len(slots))]

    pieces = probe_vectors.reshape(row_parts, part_rows, head_parts, part_width)
    pieces = pieces.transpose(2, 0, 1, 3).reshape(ctx, part_rows, part_width)
    query = lax.all_to_all(pieces, "ctx", split_axis=0, concat_axis=0, tiled=True)
    locations = sequence_locations.reshape(ctx, row_parts, part_rows)
    locations = lax.dynamic_index_in_dim(locations, i % row_parts, 1, keepdims=False)
    locations, infos = lax.optimization_barrier((locations, infos))
    attn = attention(query, locations[..., None], blocks, table)

    y, core = h // 2, h % 2
    exit_rows = total_rows // head
    depth = attention_return_matrix.shape[1]
    tiles_of = np.array(
        [
            [(1 - n // 2) * 2 + 1 - n % 2, n // 2 * 2 + 1 - n % 2]
            + [(1 - n // 2) * 2 + n % 2, n // 2 * 2 + n % 2]
            for n in range(head)
        ],
        np.int32,
    )

    def table_of(sources, tiles):
        sources = np.broadcast_to(np.stack(sources, 1)[:, None], (ctx, head, len(sources)))
        tiles = np.broadcast_to(tiles[None], (ctx, head, tiles.shape[-1]))
        return jnp.asarray(np.concatenate([sources, tiles], 2).astype(np.int32))[i, h]

    if row_parts == 1:
        way = (ctx - 1) // 2
        ring = ring_gather(moves, attn.reshape(total_rows, part_width), ctx, way, way, halves=True)
        early, late = ring[:-1], ring[-1:]
        early_info = table_of([s for s, _ in early], np.tile(np.arange(head), (head, 1)))
        late_info = table_of([s for s, _ in late], tiles_of)
        early_sum = project(
            early_info,
            [b for _, b in early],
            attention_return_matrix,
            None,
            len(early),
            head,
            exit_rows,
        )

        def finish(first, tiles):
            return project(
                late_info,
                [b for _, b in late],
                attention_return_matrix,
                early_sum,
                len(late) + first,
                tiles,
                exit_rows,
            )
    else:
        every = lax.all_gather(attn, "ctx").reshape(
            head_parts, row_parts, ctx, part_rows, part_width
        )
        every = every.transpose(2, 1, 3, 0, 4).reshape(total_rows, width_here)
        late_info = table_of([np.zeros(ctx, np.int32)], tiles_of)

        def finish(first, tiles):
            return project(
                late_info, [every], attention_return_matrix, None, 1 + first, tiles, exit_rows
            )

    give = finish(0, 2)
    far_came = moves.core_swap(give[:exit_rows])
    near_came = moves.core_swap(give[exit_rows:])
    keep = finish(2, 2)
    far_sum = keep[:exit_rows] + far_came
    mixed_rows = (keep[exit_rows:] + near_came) + moves.y_swap(far_sum)
    hidden = (skip_stream_state.astype(jnp.float32) + mixed_rows).astype(jnp.bfloat16)

    length = ctx // 2
    widened = hidden.astype(jnp.float32)
    squares = jnp.sum(widened * widened, axis=1)
    step = 2
    while step < 2 * ctx:
        bit = step if step < ctx else 1
        squares = squares + moves.ctx_move(squares, lambda n: n ^ bit)
        step *= 2
    scale = lax.rsqrt(squares / (depth * ctx) + eps)[:, None]
    far_scale = moves.y_swap(scale)

    z = i // 2
    row_args = (
        calibrating_divisor.reshape(head, exit_rows, 1),
        desired_tokens_list.reshape(head, exit_rows, 1),
    )
    waiting, normed, logits = [], [], []

    def multiply():
        slot = len(logits)
        block, across, beside, far = waiting[slot]
        after = (logits[-1:], logits[-2:-1] + normed)[slot > 1 and slot < length - 1]
        parts, _ = lax.optimization_barrier(([block, beside, across, far], after))
        own = normalize(parts, scale, far_scale, gains[slot])
        other = moves.core_swap(own)
        logits.append(
            exit_piece(
                infos[slot],
                own,
                other,
                lexicon_projection_matrix,
                logits[-1] if logits else None,
                row_args if slot == length - 1 else None,
            )
        )
        normed[:] = [own]

    def arrived(slot, block):
        across = moves.minor_swap(block)
        beside = moves.y_swap(block)
        far = moves.y_swap(across) if slot % 2 == 0 else moves.minor_swap(beside)
        waiting.append((block, across, beside, far))
        if slot == length - 2:
            multiply()
        return logits

    line_gather(moves, hidden, z, arrived)
    while len(logits) < length:
        multiply()
    logits = logits[-1]

    def in_order(pair, second):
        return jnp.where(second == 0, pair, pair[::-1])

    stats = logits[:, :3].reshape(2, 2, exit_rows, 3).transpose(3, 1, 0, 2)
    stats = in_order(stats.transpose(1, 0, 2, 3), y)
    stats = in_order(stats.transpose(2, 1, 0, 3), core)
    stats = stats.transpose(1, 2, 0, 3).reshape(3, total_rows)

    def merge(a, b):
        top = jnp.maximum(a[0], b[0])
        total = a[1] * jnp.exp(a[0] - top) + b[1] * jnp.exp(b[0] - top)
        return jnp.stack([top, total, a[2] + b[2]])

    peak, total, picked = butterfly(moves, stats, merge)
    return hidden, picked - peak - jnp.log(total)


def solution(mesh):
    placed = (
        P("ctx", "head"),
        P("ctx", "head"),
        P("ctx", "head"),
        P(),
        P("head", "ctx"),
        P("head", "ctx"),
        P("ctx"),
        P(None, ("ctx", "head")),
        P(),
        P(),
    )
    return jax.shard_map(
        functools.partial(shards, Moves(mesh)),
        mesh=mesh,
        in_specs=placed,
        out_specs=(P("head", "ctx"), P()),
        check_vma=False,
    )
```

profile of v0, /device:TPU:0, one launch (start us, length us, event | category | flops | bytes accessed | tf_op | source)
XLA Modules:
  0.0 396.2 jit_solution(15633633531529657243)
XLA Ops:
  2.1 4.1 %collective-permute-start.3 = (bf16[2,1024,128]{2,1,0:T(8,128)(2,1)S(1)}, bf16[2,1024,128]{2,1,0:T(8,128)(2,1)S(1)}, u32[]{:S(2)}, u32[]{:S(2)}) collective-permute-start(bf16[2,1024,128]{2,1,0:T(8,128)(2,1)S(1)} %pad_maximum_fusion.1), channel_id=1, source_target_pairs={{0,16},{1,17},{2,18},{3,19},{4,20},{5,21},{6,22},{7,23},{8,24},{9,... | collective-permute-start | bytes 1572872 | tf_op jit(solution)/shard_map/ppermute | solution.py:34
  6.3 1.6 collective-permute-start.1
  7.9 21.6 %collective-permute-done.3.rest_4_ = bf16[2,1024,128]{2,1,0:T(8,128)(2,1)S(1)} collective-permute-done((bf16[2,1024,128]{2,1,0:T(8,128)(2,1)S(1)}, bf16[2,1024,128]{2,1,0:T(8,128)(2,1)S(1)}, u32[]{:S(2)}, u32[]{:S(2)}) %collective-permute-start.3) | collective-permute-done | bytes 524320 | tf_op jit(solution)/shard_map/ppermute | solution.py:34
  30.1 1.5 collective-permute-start.4
  33.4 5.6 %all-to-all-start = ((bf16[8,128,256]{2,1,0:T(8,128)(2,1)}), bf16[8,128,256]{2,1,0:T(8,128)(2,1)S(1)}, u32[]{:S(2)}, u32[]{:S(2)}) async-start(bf16[8,128,256]{2,1,0:T(8,128)(2,1)} %bitcast.11), calls=%async_computation | async-start | bytes 1048576 | tf_op jit(solution)/shard_map/all_to_all | solution.py:541
  39.7 2.0 collective-permute-start.2
  41.7 3.6 collective-permute-done.5.rest_6_
  45.3 2.0 collective-permute-start.7
  49.2 28.2 %collective-permute-done.7 = bf16[1024,128]{1,0:T(8,128)(2,1)} collective-permute-done((bf16[1024,128]{1,0:T(8,128)(2,1)S(1)}, bf16[1024,128]{1,0:T(8,128)(2,1)}, u32[]{:S(2)}, u32[]{:S(2)}) %collective-permute-start.7) | collective-permute-done | bytes 262176 | tf_op jit(solution)/shard_map/ppermute | solution.py:34
  79.6 27.3 %shard_map.149 = bf16[8,128,256]{2,1,0:T(8,128)(2,1)S(1)} custom-call(s32[8]{0:T(128)S(1)} %fusion.14.table, s32[8,128,1]{2,1,0:T(8,128)S(1)} %copy.18.loc_ref, bf16[8,128,256]{2,1,0:T(8,128)(2,1)S(1)} %all-to-all-done.q_ref, bf16[2,1024,128]{2,1,0:T(8,128)(2,1)S(1)} %pad_maximum_fusion.rest_0_, bf16[2,1024,128]{2,1,0:T(8,128)(2,1)} %collective-permute-done.rest_1_, ...), custom_call_target="tpu_custom_call" | custom-call | flops 4831838208 | bytes 5242880 | tf_op jit(solution)/shard_map/pallas_call | solution.py:224
  109.0 10.7 %collective-permute-done.8.refs_1_ = bf16[1024,256]{1,0:T(8,128)(2,1)S(1)} collective-permute-done((bf16[1024,256]{1,0:T(8,128)(2,1)S(1)}, bf16[1024,256]{1,0:T(8,128)(2,1)S(1)}, u32[]{:S(2)}, u32[]{:S(2)}) %collective-permute-start.8) | collective-permute-done | bytes 524320 | tf_op jit(solution)/shard_map/ppermute | solution.py:34
  121.8 9.8 %collective-permute-done.10.refs_3_ = bf16[1024,256]{1,0:T(8,128)(2,1)S(1)} collective-permute-done((bf16[1024,256]{1,0:T(8,128)(2,1)S(1)}, bf16[1024,256]{1,0:T(8,128)(2,1)S(1)}, u32[]{:S(2)}, u32[]{:S(2)}) %collective-permute-start.10) | collective-permute-done | bytes 524320 | tf_op jit(solution)/shard_map/ppermute | solution.py:34
  131.6 1.7 collective-permute-start.12
  135.2 8.6 %collective-permute-done.12.refs_5_ = bf16[1024,256]{1,0:T(8,128)(2,1)S(1)} collective-permute-done((bf16[1024,256]{1,0:T(8,128)(2,1)S(1)}, bf16[1024,256]{1,0:T(8,128)(2,1)S(1)}, u32[]{:S(2)}, u32[]{:S(2)}) %collective-permute-start.12) | collective-permute-done | bytes 524320 | tf_op jit(solution)/shard_map/ppermute | solution.py:34
  143.8 1.5 collective-permute-start.14
  146.0 5.0 %shard_map.150.refs_0_ = f32[1024,1024]{1,0:T(8,128)S(1)} custom-call(s32[11]{0:T(128)S(1)} %fusion.13.info, bf16[1024,256]{1,0:T(8,128)(2,1)S(1)} %bitcast.75, bf16[1024,256]{1,0:T(8,128)(2,1)S(1)} %collective-permute-done.8.refs_1_, bf16[1024,256]{1,0:T(8,128)(2,1)S(1)} %collective-permute-done.9.refs_2_, ...), custom_call_target="tpu_custom_call" | custom-call | flops 3758096384 | bytes 11534336 | tf_op jit(solution)/shard_map/pallas_call | solution.py:275
  156.6 1.6 collective-permute-start.18
  159.1 22.8 %collective-permute-done.18 = f32[256,1024]{1,0:T(8,128)S(1)} collective-permute-done((f32[256,1024]{1,0:T(8,128)S(1)}, f32[256,1024]{1,0:T(8,128)S(1)}, u32[]{:S(2)}, u32[]{:S(2)}) %collective-permute-start.18) | collective-permute-done | bytes 1048608 | tf_op jit(solution)/shard_map/ppermute | solution.py:37
  183.1 1.8 collective-permute-start.24
  185.3 1.5 collective-permute-done.24
  186.9 2.9 collective-permute-start.25
  191.0 1.5 collective-permute-start.32
  192.6 1.7 collective-permute-done.20
  195.4 1.5 collective-permute-start.34
  198.0 1.6 collective-permute-start.22
  199.7 6.2 %collective-permute-done.32.refs_1_ = bf16[256,1024]{1,0:T(8,128)(2,1)S(1)} collective-permute-done((bf16[256,1024]{1,0:T(8,128)(2,1)S(1)}, bf16[256,1024]{1,0:T(8,128)(2,1)S(1)}, u32[]{:S(2)}, u32[]{:S(2)}) %collective-permute-start.32) | collective-permute-done | bytes 524320 | tf_op jit(solution)/shard_map/ppermute | solution.py:37
  206.7 8.4 %collective-permute-done.34.refs_3_ = bf16[256,1024]{1,0:T(8,128)(2,1)S(1)} collective-permute-done((bf16[256,1024]{1,0:T(8,128)(2,1)S(1)}, bf16[256,1024]{1,0:T(8,128)(2,1)S(1)}, u32[]{:S(2)}, u32[]{:S(2)}) %collective-permute-start.34) | collective-permute-done | bytes 524320 | tf_op jit(solution)/shard_map/ppermute | solution.py:37
  220.5 5.4 %collective-permute-start.29 = (bf16[256,1024]{1,0:T(8,128)(2,1)S(1)}, bf16[256,1024]{1,0:T(8,128)(2,1)}, u32[]{:S(2)}, u32[]{:S(2)}) collective-permute-start(bf16[256,1024]{1,0:T(8,128)(2,1)S(1)} %get-tuple-element.42.refs_0_), channel_id=1, source_target_pairs={{0,8},{1,9},{2,10},{3,11},{4,12},{5,13},{6,14},{7,15},{8,16},{9,17... | collective-permute-start | bytes 1572872 | tf_op jit(solution)/shard_map/ppermute | solution.py:34
  225.9 9.6 %collective-permute-done.26 = bf16[256,1024]{1,0:T(8,128)(2,1)} collective-permute-done((bf16[256,1024]{1,0:T(8,128)(2,1)S(1)}, bf16[256,1024]{1,0:T(8,128)(2,1)}, u32[]{:S(2)}, u32[]{:S(2)}) %collective-permute-start.26) | collective-permute-done | bytes 524320 | tf_op jit(solution)/shard_map/ppermute | solution.py:34
  236.8 1.5 collective-permute-start.30
  239.4 1.6 collective-permute-start.42
  241.3 9.9 %collective-permute-done.27 = bf16[256,1024]{1,0:T(8,128)(2,1)} collective-permute-done((bf16[256,1024]{1,0:T(8,128)(2,1)}, bf16[256,1024]{1,0:T(8,128)(2,1)}, u32[]{:S(2)}, u32[]{:S(2)}) %collective-permute-start.27) | collective-permute-done | bytes 524320 | tf_op jit(solution)/shard_map/ppermute | solution.py:34
  252.9 1.5 collective-permute-start.44
  254.4 13.6 %shard_map.154.rest_2_ = f32[1024,2048]{1,0:T(8,128)} custom-call(s32[7]{0:T(128)S(1)} %get-tuple-element.41.info, bf16[2,512,1024]{2,1,0:T(8,128)(2,1)S(1)} %shard_map.153.own_ref, bf16[2,512,1024]{2,1,0:T(8,128)(2,1)} %collective-permute-done.35.other_ref, bf16[8192,2048]{1,0:T(8,128)(2,1)} %rest_1_.7, bf16[8192,2048]{1,0:T(8,128)(2,1)} %rest_1_.7), custom_call_target="tpu_custom_call" | custom-call | flops 8589934592 | bytes 12582912 | tf_op jit(solution)/shard_map/pallas_call | solution.py:418
  268.1 8.6 %collective-permute-done.44.refs_3_ = bf16[256,1024]{1,0:T(8,128)(2,1)S(1)} collective-permute-done((bf16[256,1024]{1,0:T(8,128)(2,1)S(1)}, bf16[256,1024]{1,0:T(8,128)(2,1)S(1)}, u32[]{:S(2)}, u32[]{:S(2)}) %collective-permute-start.44) | collective-permute-done | bytes 524320 | tf_op jit(solution)/shard_map/ppermute | solution.py:34
  281.6 10.6 %collective-permute-done.39.refs_1_ = bf16[256,1024]{1,0:T(8,128)(2,1)S(1)} collective-permute-done((bf16[256,1024]{1,0:T(8,128)(2,1)S(1)}, bf16[256,1024]{1,0:T(8,128)(2,1)S(1)}, u32[]{:S(2)}, u32[]{:S(2)}) %collective-permute-start.39) | collective-permute-done | bytes 524320 | tf_op jit(solution)/shard_map/ppermute | solution.py:37
  292.1 10.7 %collective-permute-done.41.refs_3_ = bf16[256,1024]{1,0:T(8,128)(2,1)S(1)} collective-permute-done((bf16[256,1024]{1,0:T(8,128)(2,1)S(1)}, bf16[256,1024]{1,0:T(8,128)(2,1)S(1)}, u32[]{:S(2)}, u32[]{:S(2)}) %collective-permute-start.41) | collective-permute-done | bytes 524320 | tf_op jit(solution)/shard_map/ppermute | solution.py:37
  305.1 12.9 %collective-permute-done.36.refs_1_ = bf16[256,1024]{1,0:T(8,128)(2,1)S(1)} collective-permute-done((bf16[256,1024]{1,0:T(8,128)(2,1)S(1)}, bf16[256,1024]{1,0:T(8,128)(2,1)S(1)}, u32[]{:S(2)}, u32[]{:S(2)}) %collective-permute-start.36) | collective-permute-done | bytes 524320 | tf_op jit(solution)/shard_map/ppermute | solution.py:37
  318.3 14.4 %shard_map.157.rest_2_ = f32[1024,2048]{1,0:T(8,128)} custom-call(s32[7]{0:T(128)S(1)} %get-tuple-element.59.info, bf16[2,512,1024]{2,1,0:T(8,128)(2,1)S(1)} %shard_map.155.own_ref, bf16[2,512,1024]{2,1,0:T(8,128)(2,1)S(1)} %collective-permute-done.46.other_ref, bf16[8192,2048]{1,0:T(8,128)(2,1)} %rest_1_.7, bf16[8192,2048]{1,0:T(8,128)(2,1)} %rest_1_.7, ...), custom_call_target="tpu_custom_call" | custom-call | flops 8589934592 | bytes 12582912 | tf_op jit(solution)/shard_map/pallas_call | solution.py:418
  332.7 14.5 %shard_map.158.rest_2_ = f32[1024,2048]{1,0:T(8,128)} custom-call(s32[7]{0:T(128)S(1)} %get-tuple-element.50.info, bf16[2,512,1024]{2,1,0:T(8,128)(2,1)S(1)} %shard_map.156.own_ref, bf16[2,512,1024]{2,1,0:T(8,128)(2,1)S(1)} %collective-permute-done.45.other_ref, bf16[8192,2048]{1,0:T(8,128)(2,1)} %rest_1_.7, bf16[8192,2048]{1,0:T(8,128)(2,1)} %rest_1_.7, ...), custom_call_target="tpu_custom_call" | custom-call | flops 8589934592 | bytes 12582912 | tf_op jit(solution)/shard_map/pallas_call | solution.py:418
  348.7 3.5 collective-permute-done.47.other_ref
  352.2 19.0 %shard_map.160 = f32[1024,128]{1,0:T(8,128)S(1)} custom-call(s32[7]{0:T(128)S(1)} %get-tuple-element.34.info, bf16[2,512,1024]{2,1,0:T(8,128)(2,1)S(1)} %shard_map.159.own_ref, bf16[2,512,1024]{2,1,0:T(8,128)(2,1)} %collective-permute-done.47.other_ref, bf16[8192,2048]{1,0:T(8,128)(2,1)} %rest_1_.7, bf16[8192,2048]{1,0:T(8,128)(2,1)} %rest_1_.7, ...), custom_call_target="tpu_custom_call" | custom-call | flops 8589934592 | bytes 12582912 | tf_op jit(solution)/shard_map/pallas_call | solution.py:418
  375.9 2.6 collective-permute-done.49
  378.5 1.7 collective-permute-start.50
  380.3 2.1 collective-permute-done.50
  382.4 6.7 %collective-permute-start.51 = (f32[3,1024]{1,0:T(4,128)S(1)}, f32[3,1024]{1,0:T(4,128)S(1)}, u32[]{:S(2)}, u32[]{:S(2)}) collective-permute-start(f32[3,1024]{1,0:T(4,128)S(1)} %pad_maximum_fusion.7), channel_id=1, source_target_pairs={{0,8},{1,9},{2,10},{3,11},{4,12},{5,13},{6,14},{7,15},{8,0},{9,1},... | collective-permute-start | bytes 36872 | tf_op jit(solution)/shard_map/ppermute | solution.py:34
  389.1 1.7 collective-permute-done.51
  392.2 3.4 collective-permute-done.52
  (166 shorter events, 52.7 us)
Async XLA Ops:
  2.1 27.4 %collective-permute-start.3 = (bf16[2,1024,128]{2,1,0:T(8,128)(2,1)S(1)}, bf16[2,1024,128]{2,1,0:T(8,128)(2,1)S(1)}, u32[]{:S(2)}, u32[]{:S(2)}) collective-permute-start(bf16[2,1024,128]{2,1,0:T(8,128)(2,1)S(1)} %pad_maximum_fusion.1), channel_id=1, source_target_pairs={{0,16},{1,17},{2,18},{3,19},{4,20},{5,21},{6,22},{7,23},{8,24},{9,... | collective-permute-start | bytes 1572872 | tf_op jit(solution)/shard_map/ppermute | solution.py:34
  6.3 33.4 %collective-permute-start.1 = (bf16[2,1024,128]{2,1,0:T(8,128)(2,1)S(1)}, bf16[2,1024,128]{2,1,0:T(8,128)(2,1)}, u32[]{:S(2)}, u32[]{:S(2)}) collective-permute-start(bf16[2,1024,128]{2,1,0:T(8,128)(2,1)S(1)} %pad_maximum_fusion.rest_0_), channel_id=1, source_target_pairs={{0,8},{1,9},{2,10},{3,11},{4,12},{5,13},{6,14},{7,15},{8,0},{9,1},... | collective-permute-start | bytes 1572872 | tf_op jit(solution)/shard_map/ppermute | solution.py:34
  29.5 15.8 %collective-permute-start.5 = (bf16[2,1024,128]{2,1,0:T(8,128)(2,1)S(1)}, bf16[2,1024,128]{2,1,0:T(8,128)(2,1)S(1)}, u32[]{:S(2)}, u32[]{:S(2)}) collective-permute-start(bf16[2,1024,128]{2,1,0:T(8,128)(2,1)S(1)} %collective-permute-done.3.rest_4_), channel_id=1, source_target_pairs={{0,8},{1,9},{2,10},{3,11},{4,12},{5,13},{6,14},{7,15},{8,0},{9,1},... | collective-permute-start | bytes 1572872 | tf_op jit(solution)/shard_map/ppermute | solution.py:34
  30.1 17.3 %collective-permute-start.4 = (bf16[2,1024,128]{2,1,0:T(8,128)(2,1)S(1)}, bf16[2,1024,128]{2,1,0:T(8,128)(2,1)S(1)}, u32[]{:S(2)}, u32[]{:S(2)}) collective-permute-start(bf16[2,1024,128]{2,1,0:T(8,128)(2,1)S(1)} %collective-permute-done.3.rest_4_), channel_id=1, source_target_pairs={{0,4},{1,5},{2,6},{3,7},{4,0},{5,1},{6,2},{7,3},{8,12},{9,13},{10,... | collective-permute-start | bytes 1572872 | tf_op jit(solution)/shard_map/ppermute | solution.py:34
  31.6 47.0 %collective-permute-start = (bf16[2,1024,128]{2,1,0:T(8,128)(2,1)S(1)}, bf16[2,1024,128]{2,1,0:T(8,128)(2,1)}, u32[]{:S(2)}, u32[]{:S(2)}) collective-permute-start(bf16[2,1024,128]{2,1,0:T(8,128)(2,1)S(1)} %pad_maximum_fusion.rest_0_), channel_id=1, source_target_pairs={{0,4},{1,5},{2,6},{3,7},{4,0},{5,1},{6,2},{7,3},{8,12},{9,13},{10,... | collective-permute-start | bytes 1572872 | tf_op jit(solution)/shard_map/ppermute | solution.py:34
  33.4 45.2 %all-to-all-start = ((bf16[8,128,256]{2,1,0:T(8,128)(2,1)}), bf16[8,128,256]{2,1,0:T(8,128)(2,1)S(1)}, u32[]{:S(2)}, u32[]{:S(2)}) async-start(bf16[8,128,256]{2,1,0:T(8,128)(2,1)} %bitcast.11), calls=%async_computation | async-start | bytes 1048576 | tf_op jit(solution)/shard_map/all_to_all | solution.py:541
  39.7 38.9 %collective-permute-start.2 = (bf16[2,1024,128]{2,1,0:T(8,128)(2,1)}, bf16[2,1024,128]{2,1,0:T(8,128)(2,1)}, u32[]{:S(2)}, u32[]{:S(2)}) collective-permute-start(bf16[2,1024,128]{2,1,0:T(8,128)(2,1)} %collective-permute-done.1.rest_2_), channel_id=1, source_target_pairs={{0,4},{1,5},{2,6},{3,7},{4,0},{5,1},{6,2},{7,3},{8,12},{9,13},{10,... | collective-permute-start | bytes 1572872 | tf_op jit(solution)/shard_map/ppermute | solution.py:34
  45.3 32.1 %collective-permute-start.7 = (bf16[1024,128]{1,0:T(8,128)(2,1)S(1)}, bf16[1024,128]{1,0:T(8,128)(2,1)}, u32[]{:S(2)}, u32[]{:S(2)}) collective-permute-start(bf16[1024,128]{1,0:T(8,128)(2,1)S(1)} %slice_bitcast_fusion), channel_id=1, source_target_pairs={{0,4},{1,5},{2,6},{3,7},{4,0},{5,1},{6,2},{7,3},{8,12},{9,13},{10,... | collective-permute-start | bytes 786440 | tf_op jit(solution)/shard_map/ppermute | solution.py:34
  47.4 30.0 %collective-permute-start.6 = (bf16[1024,128]{1,0:T(8,128)(2,1)S(1)}, bf16[1024,128]{1,0:T(8,128)(2,1)}, u32[]{:S(2)}, u32[]{:S(2)}) collective-permute-start(bf16[1024,128]{1,0:T(8,128)(2,1)S(1)} %slice_bitcast_fusion.1), channel_id=1, source_target_pairs={{0,8},{1,9},{2,10},{3,11},{4,12},{5,13},{6,14},{7,15},{8,0},{9,1},... | collective-permute-start | bytes 786440 | tf_op jit(solution)/shard_map/ppermute | solution.py:34
  106.9 12.8 %collective-permute-start.8 = (bf16[1024,256]{1,0:T(8,128)(2,1)S(1)}, bf16[1024,256]{1,0:T(8,128)(2,1)S(1)}, u32[]{:S(2)}, u32[]{:S(2)}) collective-permute-start(bf16[1024,256]{1,0:T(8,128)(2,1)S(1)} %bitcast.73), channel_id=1, source_target_pairs={{0,8},{1,9},{2,10},{3,11},{4,0},{5,1},{6,2},{7,3},{8,16},{9,17},{1... | collective-permute-start | bytes 1572872 | tf_op jit(solution)/shard_map/ppermute | solution.py:34
  107.6 14.0 %collective-permute-start.9 = (bf16[1024,256]{1,0:T(8,128)(2,1)S(1)}, bf16[1024,256]{1,0:T(8,128)(2,1)S(1)}, u32[]{:S(2)}, u32[]{:S(2)}) collective-permute-start(bf16[1024,256]{1,0:T(8,128)(2,1)S(1)} %bitcast.74), channel_id=1, source_target_pairs={{0,4},{1,5},{2,6},{3,7},{4,12},{5,13},{6,14},{7,15},{8,0},{9,1},{1... | collective-permute-start | bytes 1572872 | tf_op jit(solution)/shard_map/ppermute | solution.py:34
  119.7 11.9 %collective-permute-start.10 = (bf16[1024,256]{1,0:T(8,128)(2,1)S(1)}, bf16[1024,256]{1,0:T(8,128)(2,1)S(1)}, u32[]{:S(2)}, u32[]{:S(2)}) collective-permute-start(bf16[1024,256]{1,0:T(8,128)(2,1)S(1)} %collective-permute-done.8.refs_1_), channel_id=1, source_target_pairs={{0,8},{1,9},{2,10},{3,11},{4,0},{5,1},{6,2},{7,3},{8,16},{9,17},{1... | collective-permute-start | bytes 1572872 | tf_op jit(solution)/shard_map/ppermute | solution.py:34
  121.6 12.1 %collective-permute-start.11 = (bf16[1024,256]{1,0:T(8,128)(2,1)S(1)}, bf16[1024,256]{1,0:T(8,128)(2,1)S(1)}, u32[]{:S(2)}, u32[]{:S(2)}) collective-permute-start(bf16[1024,256]{1,0:T(8,128)(2,1)S(1)} %collective-permute-done.9.refs_2_), channel_id=1, source_target_pairs={{0,4},{1,5},{2,6},{3,7},{4,12},{5,13},{6,14},{7,15},{8,0},{9,1},{1... | collective-permute-start | bytes 1572872 | tf_op jit(solution)/shard_map/ppermute | solution.py:34
  131.6 12.2 %collective-permute-start.12 = (bf16[1024,256]{1,0:T(8,128)(2,1)S(1)}, bf16[1024,256]{1,0:T(8,128)(2,1)S(1)}, u32[]{:S(2)}, u32[]{:S(2)}) collective-permute-start(bf16[1024,256]{1,0:T(8,128)(2,1)S(1)} %collective-permute-done.10.refs_3_), channel_id=1, source_target_pairs={{0,8},{1,9},{2,10},{3,11},{4,0},{5,1},{6,2},{7,3},{8,16},{9,17},{1... | collective-permute-start | bytes 1572872 | tf_op jit(solution)/shard_map/ppermute | solution.py:34
  133.7 11.9 %collective-permute-start.13 = (bf16[1024,256]{1,0:T(8,128)(2,1)S(1)}, bf16[1024,256]{1,0:T(8,128)(2,1)S(1)}, u32[]{:S(2)}, u32[]{:S(2)}) collective-permute-start(bf16[1024,256]{1,0:T(8,128)(2,1)S(1)} %collective-permute-done.11.refs_4_), channel_id=1, source_target_pairs={{0,4},{1,5},{2,6},{3,7},{4,12},{5,13},{6,14},{7,15},{8,0},{9,1},{1... | collective-permute-start | bytes 1572872 | tf_op jit(solution)/shard_map/ppermute | solution.py:34
  143.8 7.2 %collective-permute-start.14 = (bf16[512,256]{1,0:T(8,128)(2,1)S(1)}, bf16[512,256]{1,0:T(8,128)(2,1)S(1)}, u32[]{:S(2)}, u32[]{:S(2)}) collective-permute-start(bf16[512,256]{1,0:T(8,128)(2,1)S(1)} %slice.165), channel_id=1, source_target_pairs={{0,8},{1,9},{2,10},{3,11},{4,0},{5,1},{6,2},{7,3},{8,16},{9,17},{1... | collective-permute-start | bytes 786440 | tf_op jit(solution)/shard_map/ppermute | solution.py:34
  145.7 6.6 %collective-permute-start.15 = (bf16[512,256]{1,0:T(8,128)(2,1)S(1)}, bf16[512,256]{1,0:T(8,128)(2,1)S(1)}, u32[]{:S(2)}, u32[]{:S(2)}) collective-permute-start(bf16[512,256]{1,0:T(8,128)(2,1)S(1)} %slice.166), channel_id=1, source_target_pairs={{0,4},{1,5},{2,6},{3,7},{4,12},{5,13},{6,14},{7,15},{8,0},{9,1},{1... | collective-permute-start | bytes 786440 | tf_op jit(solution)/shard_map/ppermute | solution.py:34
  153.8 5.2 %collective-permute-start.16 = (f32[256,1024]{1,0:T(8,128)S(1)}, f32[256,1024]{1,0:T(8,128)S(1)}, u32[]{:S(2)}, u32[]{:S(2)}) collective-permute-start(f32[256,1024]{1,0:T(8,128)S(1)} %get-tuple-element.72), channel_id=1, source_target_pairs={{0,1},{1,0},{2,3},{3,2},{4,5},{5,4},{6,7},{7,6},{8,9},{9,8},{10,11... | collective-permute-start | bytes 3145736 | tf_op jit(solution)/shard_map/ppermute | solution.py:37
  156.6 25.3 %collective-permute-start.18 = (f32[256,1024]{1,0:T(8,128)S(1)}, f32[256,1024]{1,0:T(8,128)S(1)}, u32[]{:S(2)}, u32[]{:S(2)}) collective-permute-start(f32[256,1024]{1,0:T(8,128)S(1)} %slice_add_fusion), channel_id=1, source_target_pairs={{0,2},{1,3},{2,0},{3,1},{4,6},{5,7},{6,4},{7,5},{8,10},{9,11},{10,... | collective-permute-start | bytes 3145736 | tf_op jit(solution)/shard_map/ppermute | solution.py:37
  158.2 24.9 %collective-permute-start.23 = (f32[1,1024]{1,0:T(1,128)S(1)}, f32[1,1024]{1,0:T(1,128)S(1)}, u32[]{:S(2)}, u32[]{:S(2)}) collective-permute-start(f32[1,1024]{1,0:T(1,128)S(1)} %bitcast.79), channel_id=1, source_target_pairs={{0,4},{1,5},{2,6},{3,7},{4,0},{5,1},{6,2},{7,3},{8,12},{9,13},{10,... | collective-permute-start | bytes 12296 | tf_op jit(solution)/shard_map/ppermute | solution.py:34
  182.2 13.2 %collective-permute-start.33 = (bf16[256,1024]{1,0:T(8,128)(2,1)S(1)}, bf16[256,1024]{1,0:T(8,128)(2,1)S(1)}, u32[]{:S(2)}, u32[]{:S(2)}) collective-permute-start(bf16[256,1024]{1,0:T(8,128)(2,1)S(1)} %get-tuple-element.42.refs_0_), channel_id=1, source_target_pairs={{0,4},{1,5},{2,6},{3,7},{4,0},{5,1},{6,2},{7,3},{8,12},{9,13},{10,... | collective-permute-start | bytes 1572872 | tf_op jit(solution)/shard_map/ppermute | solution.py:34
  185.0 4.8 %collective-permute-start.19 = (f32[256]{0:T(256)S(1)}, f32[256]{0:T(256)S(1)}, u32[]{:S(2)}, u32[]{:S(2)}) collective-permute-start(f32[256]{0:T(256)S(1)} %get-tuple-element.70), channel_id=1, source_target_pairs={{0,8},{1,9},{2,10},{3,11},{4,12},{5,13},{6,14},{7,15},{8,0},{9,1},... | collective-permute-start | bytes 3080 | tf_op jit(solution)/shard_map/ppermute | solution.py:34
  186.9 10.1 %collective-permute-start.25 = (f32[4,1024]{1,0:T(4,128)S(1)}, f32[4,1024]{1,0:T(4,128)S(1)}, u32[]{:S(2)}, u32[]{:S(2)}) collective-permute-start(f32[4,1024]{1,0:T(4,128)S(1)} %pad_maximum_fusion.4), channel_id=1, source_target_pairs={{0,16},{1,17},{2,18},{3,19},{4,20},{5,21},{6,22},{7,23},{8,24},{9,... | collective-permute-start | bytes 49160 | tf_op jit(solution)/shard_map/ppermute | solution.py:34
  189.8 4.5 %collective-permute-start.20 = (f32[256]{0:T(256)S(1)}, f32[256]{0:T(256)S(1)}, u32[]{:S(2)}, u32[]{:S(2)}) collective-permute-start(f32[256]{0:T(256)S(1)} %add.139), channel_id=1, source_target_pairs={{0,16},{1,17},{2,18},{3,19},{4,20},{5,21},{6,22},{7,23},{8,24},{9,... | collective-permute-start | bytes 3080 | tf_op jit(solution)/shard_map/ppermute | solution.py:34
  191.0 14.8 %collective-permute-start.32 = (bf16[256,1024]{1,0:T(8,128)(2,1)S(1)}, bf16[256,1024]{1,0:T(8,128)(2,1)S(1)}, u32[]{:S(2)}, u32[]{:S(2)}) collective-permute-start(bf16[256,1024]{1,0:T(8,128)(2,1)S(1)} %get-tuple-element.42.refs_0_), channel_id=1, source_target_pairs={{0,2},{1,3},{2,0},{3,1},{4,6},{5,7},{6,4},{7,5},{8,10},{9,11},{10,... | collective-permute-start | bytes 1572872 | tf_op jit(solution)/shard_map/ppermute | solution.py:37
  195.4 19.7 %collective-permute-start.34 = (bf16[256,1024]{1,0:T(8,128)(2,1)S(1)}, bf16[256,1024]{1,0:T(8,128)(2,1)S(1)}, u32[]{:S(2)}, u32[]{:S(2)}) collective-permute-start(bf16[256,1024]{1,0:T(8,128)(2,1)S(1)} %collective-permute-done.33.refs_2_), channel_id=1, source_target_pairs={{0,2},{1,3},{2,0},{3,1},{4,6},{5,7},{6,4},{7,5},{8,10},{9,11},{10,... | collective-permute-start | bytes 1572872 | tf_op jit(solution)/shard_map/ppermute | solution.py:37
  198.0 18.5 %collective-permute-start.22 = (f32[256,1]{1,0:T(8,128)S(1)}, f32[256,1]{1,0:T(8,128)S(1)}, u32[]{:S(2)}, u32[]{:S(2)}) collective-permute-start(f32[256,1]{1,0:T(8,128)S(1)} %copy.23.scale_ref), channel_id=1, source_target_pairs={{0,2},{1,3},{2,0},{3,1},{4,6},{5,7},{6,4},{7,5},{8,10},{9,11},{10,... | collective-permute-start | bytes 3080 | tf_op jit(solution)/shard_map/ppermute | solution.py:37
  219.1 35.3 %collective-permute-start.35 = (bf16[2,512,1024]{2,1,0:T(8,128)(2,1)S(1)}, bf16[2,512,1024]{2,1,0:T(8,128)(2,1)}, u32[]{:S(2)}, u32[]{:S(2)}) collective-permute-start(bf16[2,512,1024]{2,1,0:T(8,128)(2,1)S(1)} %shard_map.153.own_ref), channel_id=1, source_target_pairs={{0,1},{1,0},{2,3},{3,2},{4,5},{5,4},{6,7},{7,6},{8,9},{9,8},{10,11... | collective-permute-start | bytes 6291464 | tf_op jit(solution)/shard_map/ppermute | solution.py:37
  219.2 16.3 %collective-permute-start.26 = (bf16[256,1024]{1,0:T(8,128)(2,1)S(1)}, bf16[256,1024]{1,0:T(8,128)(2,1)}, u32[]{:S(2)}, u32[]{:S(2)}) collective-permute-start(bf16[256,1024]{1,0:T(8,128)(2,1)S(1)} %get-tuple-element.42.refs_0_), channel_id=1, source_target_pairs={{8,0},{9,1},{10,2},{11,3},{12,4},{13,5},{14,6},{15,7},{16,8},{17,9... | collective-permute-start | bytes 1572872 | tf_op jit(solution)/shard_map/ppermute | solution.py:34
  220.5 16.3 %collective-permute-start.29 = (bf16[256,1024]{1,0:T(8,128)(2,1)S(1)}, bf16[256,1024]{1,0:T(8,128)(2,1)}, u32[]{:S(2)}, u32[]{:S(2)}) collective-permute-start(bf16[256,1024]{1,0:T(8,128)(2,1)S(1)} %get-tuple-element.42.refs_0_), channel_id=1, source_target_pairs={{0,8},{1,9},{2,10},{3,11},{4,12},{5,13},{6,14},{7,15},{8,16},{9,17... | collective-permute-start | bytes 1572872 | tf_op jit(solution)/shard_map/ppermute | solution.py:34
  235.5 15.7 %collective-permute-start.27 = (bf16[256,1024]{1,0:T(8,128)(2,1)}, bf16[256,1024]{1,0:T(8,128)(2,1)}, u32[]{:S(2)}, u32[]{:S(2)}) collective-permute-start(bf16[256,1024]{1,0:T(8,128)(2,1)} %collective-permute-done.26), channel_id=1, source_target_pairs={{8,0},{9,1},{10,2},{11,3},{12,4},{13,5},{14,6},{15,7},{16,8},{17,9... | collective-permute-start | bytes 1572872 | tf_op jit(solution)/shard_map/ppermute | solution.py:34
  236.8 14.4 %collective-permute-start.30 = (bf16[256,1024]{1,0:T(8,128)(2,1)}, bf16[256,1024]{1,0:T(8,128)(2,1)}, u32[]{:S(2)}, u32[]{:S(2)}) collective-permute-start(bf16[256,1024]{1,0:T(8,128)(2,1)} %collective-permute-done.29), channel_id=1, source_target_pairs={{8,16},{9,17},{10,18},{11,19},{12,20},{13,21},{14,22},{15,23},{16,... | collective-permute-start | bytes 1572872 | tf_op jit(solution)/shard_map/ppermute | solution.py:34
  239.4 13.5 %collective-permute-start.42 = (bf16[256,1024]{1,0:T(8,128)(2,1)S(1)}, bf16[256,1024]{1,0:T(8,128)(2,1)S(1)}, u32[]{:S(2)}, u32[]{:S(2)}) collective-permute-start(bf16[256,1024]{1,0:T(8,128)(2,1)S(1)} %broadcast_select_fusion.refs_0_), channel_id=1, source_target_pairs={{0,2},{1,3},{2,0},{3,1},{4,6},{5,7},{6,4},{7,5},{8,10},{9,11},{10,... | collective-permute-start | bytes 1572872 | tf_op jit(solution)/shard_map/ppermute | solution.py:37
  241.0 27.1 %collective-permute-start.43 = (bf16[256,1024]{1,0:T(8,128)(2,1)S(1)}, bf16[256,1024]{1,0:T(8,128)(2,1)S(1)}, u32[]{:S(2)}, u32[]{:S(2)}) collective-permute-start(bf16[256,1024]{1,0:T(8,128)(2,1)S(1)} %broadcast_select_fusion.refs_0_), channel_id=1, source_target_pairs={{0,4},{1,5},{2,6},{3,7},{4,0},{5,1},{6,2},{7,3},{8,12},{9,13},{10,... | collective-permute-start | bytes 1572872 | tf_op jit(solution)/shard_map/ppermute | solution.py:34
  252.3 26.1 %collective-permute-start.40 = (bf16[256,1024]{1,0:T(8,128)(2,1)S(1)}, bf16[256,1024]{1,0:T(8,128)(2,1)S(1)}, u32[]{:S(2)}, u32[]{:S(2)}) collective-permute-start(bf16[256,1024]{1,0:T(8,128)(2,1)S(1)} %select_select_fusion.1.refs_0_), channel_id=1, source_target_pairs={{0,4},{1,5},{2,6},{3,7},{4,0},{5,1},{6,2},{7,3},{8,12},{9,13},{10,... | collective-permute-start | bytes 1572872 | tf_op jit(solution)/shard_map/ppermute | solution.py:34
  252.9 23.7 %collective-permute-start.44 = (bf16[256,1024]{1,0:T(8,128)(2,1)S(1)}, bf16[256,1024]{1,0:T(8,128)(2,1)S(1)}, u32[]{:S(2)}, u32[]{:S(2)}) collective-permute-start(bf16[256,1024]{1,0:T(8,128)(2,1)S(1)} %collective-permute-done.42.refs_1_), channel_id=1, source_target_pairs={{0,4},{1,5},{2,6},{3,7},{4,0},{5,1},{6,2},{7,3},{8,12},{9,13},{10,... | collective-permute-start | bytes 1572872 | tf_op jit(solution)/shard_map/ppermute | solution.py:34
  277.2 41.1 %collective-permute-start.46 = (bf16[2,512,1024]{2,1,0:T(8,128)(2,1)S(1)}, bf16[2,512,1024]{2,1,0:T(8,128)(2,1)S(1)}, u32[]{:S(2)}, u32[]{:S(2)}) collective-permute-start(bf16[2,512,1024]{2,1,0:T(8,128)(2,1)S(1)} %shard_map.155.own_ref), channel_id=1, source_target_pairs={{0,1},{1,0},{2,3},{3,2},{4,5},{5,4},{6,7},{7,6},{8,9},{9,8},{10,11... | collective-permute-start | bytes 6291464 | tf_op jit(solution)/shard_map/ppermute | solution.py:37
  277.3 14.9 %collective-permute-start.39 = (bf16[256,1024]{1,0:T(8,128)(2,1)S(1)}, bf16[256,1024]{1,0:T(8,128)(2,1)S(1)}, u32[]{:S(2)}, u32[]{:S(2)}) collective-permute-start(bf16[256,1024]{1,0:T(8,128)(2,1)S(1)} %select_select_fusion.1.refs_0_), channel_id=1, source_target_pairs={{0,2},{1,3},{2,0},{3,1},{4,6},{5,7},{6,4},{7,5},{8,10},{9,11},{10,... | collective-permute-start | bytes 1572872 | tf_op jit(solution)/shard_map/ppermute | solution.py:37
  278.5 24.4 %collective-permute-start.41 = (bf16[256,1024]{1,0:T(8,128)(2,1)S(1)}, bf16[256,1024]{1,0:T(8,128)(2,1)S(1)}, u32[]{:S(2)}, u32[]{:S(2)}) collective-permute-start(bf16[256,1024]{1,0:T(8,128)(2,1)S(1)} %collective-permute-done.40.refs_2_), channel_id=1, source_target_pairs={{0,2},{1,3},{2,0},{3,1},{4,6},{5,7},{6,4},{7,5},{8,10},{9,11},{10,... | collective-permute-start | bytes 1572872 | tf_op jit(solution)/shard_map/ppermute | solution.py:37
  279.4 24.1 %collective-permute-start.28 = (bf16[256,1024]{1,0:T(8,128)(2,1)}, bf16[256,1024]{1,0:T(8,128)(2,1)S(1)}, u32[]{:S(2)}, u32[]{:S(2)}) collective-permute-start(bf16[256,1024]{1,0:T(8,128)(2,1)} %collective-permute-done.27), channel_id=1, source_target_pairs={{8,0},{9,1},{10,2},{11,3},{12,4},{13,5},{14,6},{15,7}} | collective-permute-start | bytes 1572872 | tf_op jit(solution)/shard_map/ppermute | solution.py:34
  280.7 22.8 %collective-permute-start.31 = (bf16[256,1024]{1,0:T(8,128)(2,1)}, bf16[256,1024]{1,0:T(8,128)(2,1)S(1)}, u32[]{:S(2)}, u32[]{:S(2)}) collective-permute-start(bf16[256,1024]{1,0:T(8,128)(2,1)} %collective-permute-done.30), channel_id=1, source_target_pairs={{16,24},{17,25},{18,26},{19,27},{20,28},{21,29},{22,30},{23,31}} | collective-permute-start | bytes 1572872 | tf_op jit(solution)/shard_map/ppermute | solution.py:34
  303.4 29.3 %collective-permute-start.45 = (bf16[2,512,1024]{2,1,0:T(8,128)(2,1)S(1)}, bf16[2,512,1024]{2,1,0:T(8,128)(2,1)S(1)}, u32[]{:S(2)}, u32[]{:S(2)}) collective-permute-start(bf16[2,512,1024]{2,1,0:T(8,128)(2,1)S(1)} %shard_map.156.own_ref), channel_id=1, source_target_pairs={{0,1},{1,0},{2,3},{3,2},{4,5},{5,4},{6,7},{7,6},{8,9},{9,8},{10,11... | collective-permute-start | bytes 6291464 | tf_op jit(solution)/shard_map/ppermute | solution.py:37
  303.6 14.4 %collective-permute-start.36 = (bf16[256,1024]{1,0:T(8,128)(2,1)S(1)}, bf16[256,1024]{1,0:T(8,128)(2,1)S(1)}, u32[]{:S(2)}, u32[]{:S(2)}) collective-permute-start(bf16[256,1024]{1,0:T(8,128)(2,1)S(1)} %select_select_fusion.refs_0_), channel_id=1, source_target_pairs={{0,2},{1,3},{2,0},{3,1},{4,6},{5,7},{6,4},{7,5},{8,10},{9,11},{10,... | collective-permute-start | bytes 1572872 | tf_op jit(solution)/shard_map/ppermute | solution.py:37
  304.8 42.5 %collective-permute-start.37 = (bf16[256,1024]{1,0:T(8,128)(2,1)S(1)}, bf16[256,1024]{1,0:T(8,128)(2,1)S(1)}, u32[]{:S(2)}, u32[]{:S(2)}) collective-permute-start(bf16[256,1024]{1,0:T(8,128)(2,1)S(1)} %select_select_fusion.refs_0_), channel_id=1, source_target_pairs={{0,4},{1,5},{2,6},{3,7},{4,0},{5,1},{6,2},{7,3},{8,12},{9,13},{10,... | collective-permute-start | bytes 1572872 | tf_op jit(solution)/shard_map/ppermute | solution.py:34
  318.0 29.3 %collective-permute-start.38 = (bf16[256,1024]{1,0:T(8,128)(2,1)S(1)}, bf16[256,1024]{1,0:T(8,128)(2,1)S(1)}, u32[]{:S(2)}, u32[]{:S(2)}) collective-permute-start(bf16[256,1024]{1,0:T(8,128)(2,1)S(1)} %collective-permute-done.36.refs_1_), channel_id=1, source_target_pairs={{0,4},{1,5},{2,6},{3,7},{4,0},{5,1},{6,2},{7,3},{8,12},{9,13},{10,... | collective-permute-start | bytes 1572872 | tf_op jit(solution)/shard_map/ppermute | solution.py:34
  347.8 4.4 %collective-permute-start.47 = (bf16[2,512,1024]{2,1,0:T(8,128)(2,1)S(1)}, bf16[2,512,1024]{2,1,0:T(8,128)(2,1)}, u32[]{:S(2)}, u32[]{:S(2)}) collective-permute-start(bf16[2,512,1024]{2,1,0:T(8,128)(2,1)S(1)} %shard_map.159.own_ref), channel_id=1, source_target_pairs={{0,1},{1,0},{2,3},{3,2},{4,5},{5,4},{6,7},{7,6},{8,9},{9,8},{10,11... | collective-permute-start | bytes 6291464 | tf_op jit(solution)/shard_map/ppermute | solution.py:37
  382.4 8.4 %collective-permute-start.51 = (f32[3,1024]{1,0:T(4,128)S(1)}, f32[3,1024]{1,0:T(4,128)S(1)}, u32[]{:S(2)}, u32[]{:S(2)}) collective-permute-start(f32[3,1024]{1,0:T(4,128)S(1)} %pad_maximum_fusion.7), channel_id=1, source_target_pairs={{0,8},{1,9},{2,10},{3,11},{4,12},{5,13},{6,14},{7,15},{8,0},{9,1},... | collective-permute-start | bytes 36872 | tf_op jit(solution)/shard_map/ppermute | solution.py:34
  390.8 4.7 %collective-permute-start.52 = (f32[3,1024]{1,0:T(4,128)S(1)}, f32[3,1024]{1,0:T(4,128)S(1)}, u32[]{:S(2)}, u32[]{:S(2)}) collective-permute-start(f32[3,1024]{1,0:T(4,128)S(1)} %pad_maximum_fusion.8), channel_id=1, source_target_pairs={{0,16},{1,17},{2,18},{3,19},{4,20},{5,21},{6,22},{7,23},{8,24},{9,... | collective-permute-start | bytes 36872 | tf_op jit(solution)/shard_map/ppermute | solution.py:34
  (21 other events, 251.4 us)
where the time goes:
time: 397 us; the launch traced here: 396 us
  waiting for transfers between devices  205 us (52%)
  Pallas kernels  98.5 us (25%)
  starting transfers between devices  72.1 us (18%)
  local copies, waits for them, and re-layouts  14.5 us (4%)
  other arithmetic  4.94 us (1%)
    ppermute x37, waiting for transfers between devices, ctx_move(): return lax.ppermute(value, AXES, self.perm(ctx_to=ctx_to))  124 us
    ppermute x16, waiting for transfers between devices, head_move(): return lax.ppermute(value, AXES, self.perm(head_to=head_to))  80.5 us
    pallas_call x4, Pallas kernels, exit_piece(): pl.pallas_call(functools.partial(exit_kernel, final, before is not None),...  61.6 us
    ppermute x37, starting transfers between devices, ctx_move(): return lax.ppermute(value, AXES, self.perm(ctx_to=ctx_to))  53.2 us
    pallas_call x1, Pallas kernels, attention(): pl.pallas_call(functools.partial(attention_kernel, count, heads), out_sha...  27.3 us
    ppermute x16, starting transfers between devices, head_move(): return lax.ppermute(value, AXES, self.perm(head_to=head_to))  13.3 us
  transfers between devices with their start and end apart: 54, of which 32 were waited for; matrix products, arithmetic and copies ran while one was open for 3% of the time, Pallas kernels for 13%

commit v1 on v0

--- a/solution.py
+++ b/solution.py
@@ -95,7 +95,7 @@
     kept_xz = move(kept_z, 1)
     came_x = move(came, 1)
     came_z = move(came, 2)
-    far = jnp.stack([move(came_x[0], 2), move(came_z[1], 1)])
+    far = move(came_x, 2)
     return (
         [(origin(0), kept), (origin(1), kept_x), (origin(2), kept_z), (origin(3), kept_xz)],
         [(origin(0), came), (origin(1), came_x), (origin(2), came_z), (origin(3), far)],
@@ -623,12 +623,12 @@
         calibrating_divisor.reshape(head, exit_rows, 1),
         desired_tokens_list.reshape(head, exit_rows, 1),
     )
-    waiting, normed, logits = [], [], []
+    waiting, logits = [], []
 
     def multiply():
         slot = len(logits)
         block, across, beside, far = waiting[slot]
-        after = (logits[-1:], logits[-2:-1] + normed)[slot > 1 and slot < length - 1]
+        after = (logits[-2:-1] if 1 < slot < length - 1 else logits[-1:]) or [waiting[-1][0]]
         parts, _ = lax.optimization_barrier(([block, beside, across, far], after))
         own = normalize(parts, scale, far_scale, gains[slot])
         other = moves.core_swap(own)
@@ -642,7 +642,6 @@
                 row_args if slot == length - 1 else None,
             )
         )
-        normed[:] = [own]
 
     def arrived(slot, block):
         across = moves.minor_swap(block)

time: 397 us -> 382 us (0.962)
  waiting for transfers between devices: 205 us -> 198 us
  local copies, waits for them, and re-layouts: 14.5 us -> 9.69 us
    ppermute x37 -> x36, waiting for transfers between devices: 124 us -> 113 us  [ctx_move(): return lax.ppermute(value, AXES, self.perm(ctx_to=ctx_to))]
    ppermute x16, waiting for transfers between devices: 80.5 us -> 85.7 us  [head_move(): return lax.ppermute(value, AXES, self.perm(head_to=head_to))]
    unnamed x36 -> x24, local copies, waits for them, and re-layouts: 5.95 us -> 1.16 us
    ppermute x37 -> x36, starting transfers between devices: 53.2 us -> 56.6 us  [ctx_move(): return lax.ppermute(value, AXES, self.perm(ctx_to=ctx_to))]
  transfers between devices with their start and end apart: 54 -> 53, of which waited for: 32 -> 29; matrix products, arithmetic and copies ran while one was open for 3% -> 2% of each run, Pallas kernels for 13% -> 13%
where the time goes in v1:
time: 382 us; the launch traced here: 381 us
  waiting for transfers between devices  198 us (52%)
  Pallas kernels  97.9 us (26%)
  starting transfers between devices  72.3 us (19%)
  local copies, waits for them, and re-layouts  9.69 us (3%)
    ppermute x36, waiting for transfers between devices, ctx_move(): return lax.ppermute(value, AXES, self.perm(ctx_to=ctx_to))  113 us
    ppermute x16, waiting for transfers between devices, head_move(): return lax.ppermute(value, AXES, self.perm(head_to=head_to))  85.7 us
    pallas_call x4, Pallas kernels, exit_piece(): pl.pallas_call(functools.partial(exit_kernel, final, before is not None),...  60.7 us
    ppermute x36, starting transfers between devices, ctx_move(): return lax.ppermute(value, AXES, self.perm(ctx_to=ctx_to))  56.6 us
    pallas_call x1, Pallas kernels, attention(): pl.pallas_call(functools.partial(attention_kernel, count, heads), out_sha...  27.6 us
    ppermute x16, starting transfers between devices, head_move(): return lax.ppermute(value, AXES, self.perm(head_to=head_to))  11.1 us
  transfers between devices with their start and end apart: 53, of which 29 were waited for; matrix products, arithmetic and copies ran while one was open for 2% of the time, Pallas kernels for 13%

profile of v1, /device:TPU:0, one launch (start us, length us, event | category | flops | bytes accessed | tf_op | source)
XLA Modules:
  0.0 381.4 jit_solution(145794195677371039)
XLA Ops:
  2.1 4.1 %collective-permute-start.3 = (bf16[2,1024,128]{2,1,0:T(8,128)(2,1)S(1)}, bf16[2,1024,128]{2,1,0:T(8,128)(2,1)S(1)}, u32[]{:S(2)}, u32[]{:S(2)}) collective-permute-start(bf16[2,1024,128]{2,1,0:T(8,128)(2,1)S(1)} %pad_maximum_fusion.1), channel_id=1, source_target_pairs={{0,16},{1,17},{2,18},{3,19},{4,20},{5,21},{6,22},{7,23},{8,24},{9,... | collective-permute-start | bytes 1572872 | tf_op jit(solution)/shard_map/ppermute | solution.py:34
  6.2 1.6 collective-permute-start.1
  7.9 21.6 %collective-permute-done.3.rest_4_ = bf16[2,1024,128]{2,1,0:T(8,128)(2,1)S(1)} collective-permute-done((bf16[2,1024,128]{2,1,0:T(8,128)(2,1)S(1)}, bf16[2,1024,128]{2,1,0:T(8,128)(2,1)S(1)}, u32[]{:S(2)}, u32[]{:S(2)}) %collective-permute-start.3) | collective-permute-done | bytes 524320 | tf_op jit(solution)/shard_map/ppermute | solution.py:34
  29.5 1.5 collective-permute-start.4
  32.3 4.7 %all-to-all-start = ((bf16[8,128,256]{2,1,0:T(8,128)(2,1)}), bf16[8,128,256]{2,1,0:T(8,128)(2,1)S(1)}, u32[]{:S(2)}, u32[]{:S(2)}) async-start(bf16[8,128,256]{2,1,0:T(8,128)(2,1)} %bitcast.11), calls=%async_computation | async-start | bytes 1048576 | tf_op jit(solution)/shard_map/all_to_all | solution.py:541
  37.0 2.0 collective-permute-start
  41.0 6.9 %collective-permute-done.4.rest_5_ = bf16[2,1024,128]{2,1,0:T(8,128)(2,1)} collective-permute-done((bf16[2,1024,128]{2,1,0:T(8,128)(2,1)S(1)}, bf16[2,1024,128]{2,1,0:T(8,128)(2,1)}, u32[]{:S(2)}, u32[]{:S(2)}) %collective-permute-start.4) | collective-permute-done | bytes 524320 | tf_op jit(solution)/shard_map/ppermute | solution.py:34
  49.5 11.7 %collective-permute-done.rest_1_ = bf16[2,1024,128]{2,1,0:T(8,128)(2,1)} collective-permute-done((bf16[2,1024,128]{2,1,0:T(8,128)(2,1)S(1)}, bf16[2,1024,128]{2,1,0:T(8,128)(2,1)}, u32[]{:S(2)}, u32[]{:S(2)}) %collective-permute-start) | collective-permute-done | bytes 524320 | tf_op jit(solution)/shard_map/ppermute | solution.py:34
  61.2 9.5 %collective-permute-done.2.rest_3_ = bf16[2,1024,128]{2,1,0:T(8,128)(2,1)} collective-permute-done((bf16[2,1024,128]{2,1,0:T(8,128)(2,1)S(1)}, bf16[2,1024,128]{2,1,0:T(8,128)(2,1)}, u32[]{:S(2)}, u32[]{:S(2)}) %collective-permute-start.2) | collective-permute-done | bytes 524320 | tf_op jit(solution)/shard_map/ppermute | solution.py:34
  70.7 27.6 %shard_map.149 = bf16[8,128,256]{2,1,0:T(8,128)(2,1)S(1)} custom-call(s32[8]{0:T(128)S(1)} %fusion.14.table, s32[8,128,1]{2,1,0:T(8,128)S(1)} %copy.18.loc_ref, bf16[8,128,256]{2,1,0:T(8,128)(2,1)S(1)} %all-to-all-done.q_ref, bf16[2,1024,128]{2,1,0:T(8,128)(2,1)S(1)} %pad_maximum_fusion.rest_0_, bf16[2,1024,128]{2,1,0:T(8,128)(2,1)} %collective-permute-done.rest_1_, ...), custom_call_target="tpu_custom_call" | custom-call | flops 4831838208 | bytes 5242880 | tf_op jit(solution)/shard_map/pallas_call | solution.py:224
  100.4 10.2 %collective-permute-done.7.refs_1_ = bf16[1024,256]{1,0:T(8,128)(2,1)S(1)} collective-permute-done((bf16[1024,256]{1,0:T(8,128)(2,1)S(1)}, bf16[1024,256]{1,0:T(8,128)(2,1)S(1)}, u32[]{:S(2)}, u32[]{:S(2)}) %collective-permute-start.7) | collective-permute-done | bytes 524320 | tf_op jit(solution)/shard_map/ppermute | solution.py:34
  110.6 2.2 collective-permute-start.9
  112.8 10.0 %collective-permute-done.9.refs_3_ = bf16[1024,256]{1,0:T(8,128)(2,1)S(1)} collective-permute-done((bf16[1024,256]{1,0:T(8,128)(2,1)S(1)}, bf16[1024,256]{1,0:T(8,128)(2,1)S(1)}, u32[]{:S(2)}, u32[]{:S(2)}) %collective-permute-start.9) | collective-permute-done | bytes 524320 | tf_op jit(solution)/shard_map/ppermute | solution.py:34
  122.8 2.1 collective-permute-start.11
  126.5 8.0 %collective-permute-done.11.refs_5_ = bf16[1024,256]{1,0:T(8,128)(2,1)S(1)} collective-permute-done((bf16[1024,256]{1,0:T(8,128)(2,1)S(1)}, bf16[1024,256]{1,0:T(8,128)(2,1)S(1)}, u32[]{:S(2)}, u32[]{:S(2)}) %collective-permute-start.11) | collective-permute-done | bytes 524320 | tf_op jit(solution)/shard_map/ppermute | solution.py:34
  134.5 2.5 collective-permute-start.13
  137.5 5.1 %shard_map.150.refs_0_ = f32[1024,1024]{1,0:T(8,128)S(1)} custom-call(s32[11]{0:T(128)S(1)} %fusion.13.info, bf16[1024,256]{1,0:T(8,128)(2,1)S(1)} %bitcast.69, bf16[1024,256]{1,0:T(8,128)(2,1)S(1)} %collective-permute-done.7.refs_1_, bf16[1024,256]{1,0:T(8,128)(2,1)S(1)} %collective-permute-done.8.refs_2_, ...), custom_call_target="tpu_custom_call" | custom-call | flops 3758096384 | bytes 11534336 | tf_op jit(solution)/shard_map/pallas_call | solution.py:275
  148.0 1.6 collective-permute-start.17
  150.5 2.6 collective-permute-done.22
  153.1 1.9 collective-permute-start.23
  155.0 18.2 %collective-permute-done.17 = f32[256,1024]{1,0:T(8,128)S(1)} collective-permute-done((f32[256,1024]{1,0:T(8,128)S(1)}, f32[256,1024]{1,0:T(8,128)S(1)}, u32[]{:S(2)}, u32[]{:S(2)}) %collective-permute-start.17) | collective-permute-done | bytes 1048608 | tf_op jit(solution)/shard_map/ppermute | solution.py:37
  174.8 4.6 %collective-permute-start.28 = (bf16[256,1024]{1,0:T(8,128)(2,1)S(1)}, bf16[256,1024]{1,0:T(8,128)(2,1)S(1)}, u32[]{:S(2)}, u32[]{:S(2)}) collective-permute-start(bf16[256,1024]{1,0:T(8,128)(2,1)S(1)} %get-tuple-element.42.refs_0_), channel_id=1, source_target_pairs={{0,8},{1,9},{2,10},{3,11},{4,12},{5,13},{6,14},{7,15},{8,16},{9,17... | collective-permute-start | bytes 1572872 | tf_op jit(solution)/shard_map/ppermute | solution.py:34
  179.5 3.3 collective-permute-start.24
  183.8 6.4 %collective-permute-done.18 = f32[256]{0:T(256)S(1)} collective-permute-done((f32[256]{0:T(256)S(1)}, f32[256]{0:T(256)S(1)}, u32[]{:S(2)}, u32[]{:S(2)}) %collective-permute-start.18) | collective-permute-done | bytes 1056 | tf_op jit(solution)/shard_map/ppermute | solution.py:34
  190.2 3.0 collective-permute-start.19
  198.6 1.6 collective-permute-start.31
  200.9 1.5 collective-permute-start.33
  202.5 6.6 %collective-permute-done.26 = bf16[256,1024]{1,0:T(8,128)(2,1)S(1)} collective-permute-done((bf16[256,1024]{1,0:T(8,128)(2,1)S(1)}, bf16[256,1024]{1,0:T(8,128)(2,1)S(1)}, u32[]{:S(2)}, u32[]{:S(2)}) %collective-permute-start.26) | collective-permute-done | bytes 524320 | tf_op jit(solution)/shard_map/ppermute | solution.py:34
  209.3 4.2 %collective-permute-done.31.refs_1_ = bf16[256,1024]{1,0:T(8,128)(2,1)S(1)} collective-permute-done((bf16[256,1024]{1,0:T(8,128)(2,1)S(1)}, bf16[256,1024]{1,0:T(8,128)(2,1)S(1)}, u32[]{:S(2)}, u32[]{:S(2)}) %collective-permute-start.31) | collective-permute-done | bytes 524320 | tf_op jit(solution)/shard_map/ppermute | solution.py:37
  213.4 10.0 %collective-permute-done.33.refs_3_ = bf16[256,1024]{1,0:T(8,128)(2,1)S(1)} collective-permute-done((bf16[256,1024]{1,0:T(8,128)(2,1)S(1)}, bf16[256,1024]{1,0:T(8,128)(2,1)S(1)}, u32[]{:S(2)}, u32[]{:S(2)}) %collective-permute-start.33) | collective-permute-done | bytes 524320 | tf_op jit(solution)/shard_map/ppermute | solution.py:37
  224.0 1.6 collective-permute-start.42
  227.6 10.7 %collective-permute-done.42.refs_1_ = bf16[256,1024]{1,0:T(8,128)(2,1)S(1)} collective-permute-done((bf16[256,1024]{1,0:T(8,128)(2,1)S(1)}, bf16[256,1024]{1,0:T(8,128)(2,1)S(1)}, u32[]{:S(2)}, u32[]{:S(2)}) %collective-permute-start.42) | collective-permute-done | bytes 524320 | tf_op jit(solution)/shard_map/ppermute | solution.py:37
  239.3 12.9 %shard_map.154.rest_2_ = f32[1024,2048]{1,0:T(8,128)} custom-call(s32[7]{0:T(128)S(1)} %get-tuple-element.41.info, bf16[2,512,1024]{2,1,0:T(8,128)(2,1)S(1)} %shard_map.153.own_ref, bf16[2,512,1024]{2,1,0:T(8,128)(2,1)S(1)} %collective-permute-done.34.other_ref, bf16[8192,2048]{1,0:T(8,128)(2,1)} %rest_1_.7, bf16[8192,2048]{1,0:T(8,128)(2,1)} %rest_1_.7), custom_call_target="tpu_custom_call" | custom-call | flops 8589934592 | bytes 12582912 | tf_op jit(solution)/shard_map/pallas_call | solution.py:418
  252.3 9.8 %collective-permute-done.44.refs_3_ = bf16[256,1024]{1,0:T(8,128)(2,1)S(1)} collective-permute-done((bf16[256,1024]{1,0:T(8,128)(2,1)S(1)}, bf16[256,1024]{1,0:T(8,128)(2,1)S(1)}, u32[]{:S(2)}, u32[]{:S(2)}) %collective-permute-start.44) | collective-permute-done | bytes 524320 | tf_op jit(solution)/shard_map/ppermute | solution.py:34
  263.3 1.5 collective-permute-start.40
  267.0 10.6 %collective-permute-done.38.refs_1_ = bf16[256,1024]{1,0:T(8,128)(2,1)S(1)} collective-permute-done((bf16[256,1024]{1,0:T(8,128)(2,1)S(1)}, bf16[256,1024]{1,0:T(8,128)(2,1)S(1)}, u32[]{:S(2)}, u32[]{:S(2)}) %collective-permute-start.38) | collective-permute-done | bytes 524320 | tf_op jit(solution)/shard_map/ppermute | solution.py:37
  277.6 10.7 %collective-permute-done.40.refs_3_ = bf16[256,1024]{1,0:T(8,128)(2,1)S(1)} collective-permute-done((bf16[256,1024]{1,0:T(8,128)(2,1)S(1)}, bf16[256,1024]{1,0:T(8,128)(2,1)S(1)}, u32[]{:S(2)}, u32[]{:S(2)}) %collective-permute-start.40) | collective-permute-done | bytes 524320 | tf_op jit(solution)/shard_map/ppermute | solution.py:37
  290.6 12.8 %collective-permute-done.35.refs_1_ = bf16[256,1024]{1,0:T(8,128)(2,1)S(1)} collective-permute-done((bf16[256,1024]{1,0:T(8,128)(2,1)S(1)}, bf16[256,1024]{1,0:T(8,128)(2,1)S(1)}, u32[]{:S(2)}, u32[]{:S(2)}) %collective-permute-start.35) | collective-permute-done | bytes 524320 | tf_op jit(solution)/shard_map/ppermute | solution.py:37
  304.4 14.4 %shard_map.157.rest_2_ = f32[1024,2048]{1,0:T(8,128)} custom-call(s32[7]{0:T(128)S(1)} %get-tuple-element.55.info, bf16[2,512,1024]{2,1,0:T(8,128)(2,1)S(1)} %shard_map.156.own_ref, bf16[2,512,1024]{2,1,0:T(8,128)(2,1)S(1)} %collective-permute-done.45.other_ref, bf16[8192,2048]{1,0:T(8,128)(2,1)} %rest_1_.7, bf16[8192,2048]{1,0:T(8,128)(2,1)} %rest_1_.7, ...), custom_call_target="tpu_custom_call" | custom-call | flops 8589934592 | bytes 12582912 | tf_op jit(solution)/shard_map/pallas_call | solution.py:418
  318.8 14.4 %shard_map.158.rest_2_ = f32[1024,2048]{1,0:T(8,128)} custom-call(s32[7]{0:T(128)S(1)} %get-tuple-element.50.info, bf16[2,512,1024]{2,1,0:T(8,128)(2,1)S(1)} %shard_map.155.own_ref, bf16[2,512,1024]{2,1,0:T(8,128)(2,1)S(1)} %collective-permute-done.41.other_ref, bf16[8192,2048]{1,0:T(8,128)(2,1)} %rest_1_.7, bf16[8192,2048]{1,0:T(8,128)(2,1)} %rest_1_.7, ...), custom_call_target="tpu_custom_call" | custom-call | flops 8589934592 | bytes 12582912 | tf_op jit(solution)/shard_map/pallas_call | solution.py:418
  334.7 3.5 collective-permute-done.46.other_ref
  338.2 18.9 %shard_map.160 = f32[1024,128]{1,0:T(8,128)S(1)} custom-call(s32[7]{0:T(128)S(1)} %get-tuple-element.34.info, bf16[2,512,1024]{2,1,0:T(8,128)(2,1)S(1)} %shard_map.159.own_ref, bf16[2,512,1024]{2,1,0:T(8,128)(2,1)} %collective-permute-done.46.other_ref, bf16[8192,2048]{1,0:T(8,128)(2,1)} %rest_1_.7, bf16[8192,2048]{1,0:T(8,128)(2,1)} %rest_1_.7, ...), custom_call_target="tpu_custom_call" | custom-call | flops 8589934592 | bytes 12582912 | tf_op jit(solution)/shard_map/pallas_call | solution.py:418
  361.3 3.2 collective-permute-done.48
  365.6 2.7 collective-permute-done.49
  368.4 5.9 %collective-permute-start.50 = (f32[3,1024]{1,0:T(4,128)S(1)}, f32[3,1024]{1,0:T(4,128)S(1)}, u32[]{:S(2)}, u32[]{:S(2)}) collective-permute-start(f32[3,1024]{1,0:T(4,128)S(1)} %pad_maximum_fusion.6), channel_id=1, source_target_pairs={{0,8},{1,9},{2,10},{3,11},{4,12},{5,13},{6,14},{7,15},{8,0},{9,1},... | collective-permute-start | bytes 36872 | tf_op jit(solution)/shard_map/ppermute | solution.py:34
  374.3 1.7 collective-permute-done.50
  376.0 2.1 collective-permute-start.51
  378.1 2.6 collective-permute-done.51
  (149 shorter events, 43.3 us)
Async XLA Ops:
  2.1 27.4 %collective-permute-start.3 = (bf16[2,1024,128]{2,1,0:T(8,128)(2,1)S(1)}, bf16[2,1024,128]{2,1,0:T(8,128)(2,1)S(1)}, u32[]{:S(2)}, u32[]{:S(2)}) collective-permute-start(bf16[2,1024,128]{2,1,0:T(8,128)(2,1)S(1)} %pad_maximum_fusion.1), channel_id=1, source_target_pairs={{0,16},{1,17},{2,18},{3,19},{4,20},{5,21},{6,22},{7,23},{8,24},{9,... | collective-permute-start | bytes 1572872 | tf_op jit(solution)/shard_map/ppermute | solution.py:34
  6.2 34.2 %collective-permute-start.1 = (bf16[2,1024,128]{2,1,0:T(8,128)(2,1)S(1)}, bf16[2,1024,128]{2,1,0:T(8,128)(2,1)S(1)}, u32[]{:S(2)}, u32[]{:S(2)}) collective-permute-start(bf16[2,1024,128]{2,1,0:T(8,128)(2,1)S(1)} %pad_maximum_fusion.rest_0_), channel_id=1, source_target_pairs={{0,8},{1,9},{2,10},{3,11},{4,12},{5,13},{6,14},{7,15},{8,0},{9,1},... | collective-permute-start | bytes 1572872 | tf_op jit(solution)/shard_map/ppermute | solution.py:34
  29.5 18.4 %collective-permute-start.4 = (bf16[2,1024,128]{2,1,0:T(8,128)(2,1)S(1)}, bf16[2,1024,128]{2,1,0:T(8,128)(2,1)}, u32[]{:S(2)}, u32[]{:S(2)}) collective-permute-start(bf16[2,1024,128]{2,1,0:T(8,128)(2,1)S(1)} %collective-permute-done.3.rest_4_), channel_id=1, source_target_pairs={{0,4},{1,5},{2,6},{3,7},{4,0},{5,1},{6,2},{7,3},{8,12},{9,13},{10,... | collective-permute-start | bytes 1572872 | tf_op jit(solution)/shard_map/ppermute | solution.py:34
  32.3 28.9 %all-to-all-start = ((bf16[8,128,256]{2,1,0:T(8,128)(2,1)}), bf16[8,128,256]{2,1,0:T(8,128)(2,1)S(1)}, u32[]{:S(2)}, u32[]{:S(2)}) async-start(bf16[8,128,256]{2,1,0:T(8,128)(2,1)} %bitcast.11), calls=%async_computation | async-start | bytes 1048576 | tf_op jit(solution)/shard_map/all_to_all | solution.py:541
  37.0 24.3 %collective-permute-start = (bf16[2,1024,128]{2,1,0:T(8,128)(2,1)S(1)}, bf16[2,1024,128]{2,1,0:T(8,128)(2,1)}, u32[]{:S(2)}, u32[]{:S(2)}) collective-permute-start(bf16[2,1024,128]{2,1,0:T(8,128)(2,1)S(1)} %pad_maximum_fusion.rest_0_), channel_id=1, source_target_pairs={{0,4},{1,5},{2,6},{3,7},{4,0},{5,1},{6,2},{7,3},{8,12},{9,13},{10,... | collective-permute-start | bytes 1572872 | tf_op jit(solution)/shard_map/ppermute | solution.py:34
  39.0 31.7 %collective-permute-start.5 = (bf16[2,1024,128]{2,1,0:T(8,128)(2,1)S(1)}, bf16[2,1024,128]{2,1,0:T(8,128)(2,1)}, u32[]{:S(2)}, u32[]{:S(2)}) collective-permute-start(bf16[2,1024,128]{2,1,0:T(8,128)(2,1)S(1)} %collective-permute-done.3.rest_4_), channel_id=1, source_target_pairs={{0,8},{1,9},{2,10},{3,11},{4,12},{5,13},{6,14},{7,15},{8,0},{9,1},... | collective-permute-start | bytes 1572872 | tf_op jit(solution)/shard_map/ppermute | solution.py:34
  40.4 30.2 %collective-permute-start.2 = (bf16[2,1024,128]{2,1,0:T(8,128)(2,1)S(1)}, bf16[2,1024,128]{2,1,0:T(8,128)(2,1)}, u32[]{:S(2)}, u32[]{:S(2)}) collective-permute-start(bf16[2,1024,128]{2,1,0:T(8,128)(2,1)S(1)} %collective-permute-done.1.rest_2_), channel_id=1, source_target_pairs={{0,4},{1,5},{2,6},{3,7},{4,0},{5,1},{6,2},{7,3},{8,12},{9,13},{10,... | collective-permute-start | bytes 1572872 | tf_op jit(solution)/shard_map/ppermute | solution.py:34
  47.9 22.8 %collective-permute-start.6 = (bf16[2,1024,128]{2,1,0:T(8,128)(2,1)}, bf16[2,1024,128]{2,1,0:T(8,128)(2,1)}, u32[]{:S(2)}, u32[]{:S(2)}) collective-permute-start(bf16[2,1024,128]{2,1,0:T(8,128)(2,1)} %collective-permute-done.4.rest_5_), channel_id=1, source_target_pairs={{0,8},{1,9},{2,10},{3,11},{4,12},{5,13},{6,14},{7,15},{8,0},{9,1},... | collective-permute-start | bytes 1572872 | tf_op jit(solution)/shard_map/ppermute | solution.py:34
  98.3 12.3 %collective-permute-start.7 = (bf16[1024,256]{1,0:T(8,128)(2,1)S(1)}, bf16[1024,256]{1,0:T(8,128)(2,1)S(1)}, u32[]{:S(2)}, u32[]{:S(2)}) collective-permute-start(bf16[1024,256]{1,0:T(8,128)(2,1)S(1)} %bitcast.67), channel_id=1, source_target_pairs={{0,8},{1,9},{2,10},{3,11},{4,0},{5,1},{6,2},{7,3},{8,16},{9,17},{1... | collective-permute-start | bytes 1572872 | tf_op jit(solution)/shard_map/ppermute | solution.py:34
  99.8 13.0 %collective-permute-start.8 = (bf16[1024,256]{1,0:T(8,128)(2,1)S(1)}, bf16[1024,256]{1,0:T(8,128)(2,1)S(1)}, u32[]{:S(2)}, u32[]{:S(2)}) collective-permute-start(bf16[1024,256]{1,0:T(8,128)(2,1)S(1)} %bitcast.68), channel_id=1, source_target_pairs={{0,4},{1,5},{2,6},{3,7},{4,12},{5,13},{6,14},{7,15},{8,0},{9,1},{1... | collective-permute-start | bytes 1572872 | tf_op jit(solution)/shard_map/ppermute | solution.py:34
  110.6 12.2 %collective-permute-start.9 = (bf16[1024,256]{1,0:T(8,128)(2,1)S(1)}, bf16[1024,256]{1,0:T(8,128)(2,1)S(1)}, u32[]{:S(2)}, u32[]{:S(2)}) collective-permute-start(bf16[1024,256]{1,0:T(8,128)(2,1)S(1)} %collective-permute-done.7.refs_1_), channel_id=1, source_target_pairs={{0,8},{1,9},{2,10},{3,11},{4,0},{5,1},{6,2},{7,3},{8,16},{9,17},{1... | collective-permute-start | bytes 1572872 | tf_op jit(solution)/shard_map/ppermute | solution.py:34
  112.8 12.3 %collective-permute-start.10 = (bf16[1024,256]{1,0:T(8,128)(2,1)S(1)}, bf16[1024,256]{1,0:T(8,128)(2,1)S(1)}, u32[]{:S(2)}, u32[]{:S(2)}) collective-permute-start(bf16[1024,256]{1,0:T(8,128)(2,1)S(1)} %collective-permute-done.8.refs_2_), channel_id=1, source_target_pairs={{0,4},{1,5},{2,6},{3,7},{4,12},{5,13},{6,14},{7,15},{8,0},{9,1},{1... | collective-permute-start | bytes 1572872 | tf_op jit(solution)/shard_map/ppermute | solution.py:34
  122.8 11.6 %collective-permute-start.11 = (bf16[1024,256]{1,0:T(8,128)(2,1)S(1)}, bf16[1024,256]{1,0:T(8,128)(2,1)S(1)}, u32[]{:S(2)}, u32[]{:S(2)}) collective-permute-start(bf16[1024,256]{1,0:T(8,128)(2,1)S(1)} %collective-permute-done.9.refs_3_), channel_id=1, source_target_pairs={{0,8},{1,9},{2,10},{3,11},{4,0},{5,1},{6,2},{7,3},{8,16},{9,17},{1... | collective-permute-start | bytes 1572872 | tf_op jit(solution)/shard_map/ppermute | solution.py:34
  125.1 12.0 %collective-permute-start.12 = (bf16[1024,256]{1,0:T(8,128)(2,1)S(1)}, bf16[1024,256]{1,0:T(8,128)(2,1)S(1)}, u32[]{:S(2)}, u32[]{:S(2)}) collective-permute-start(bf16[1024,256]{1,0:T(8,128)(2,1)S(1)} %collective-permute-done.10.refs_4_), channel_id=1, source_target_pairs={{0,4},{1,5},{2,6},{3,7},{4,12},{5,13},{6,14},{7,15},{8,0},{9,1},{1... | collective-permute-start | bytes 1572872 | tf_op jit(solution)/shard_map/ppermute | solution.py:34
  134.5 8.0 %collective-permute-start.13 = (bf16[512,256]{1,0:T(8,128)(2,1)S(1)}, bf16[512,256]{1,0:T(8,128)(2,1)S(1)}, u32[]{:S(2)}, u32[]{:S(2)}) collective-permute-start(bf16[512,256]{1,0:T(8,128)(2,1)S(1)} %slice.155), channel_id=1, source_target_pairs={{0,8},{1,9},{2,10},{3,11},{4,0},{5,1},{6,2},{7,3},{8,16},{9,17},{1... | collective-permute-start | bytes 786440 | tf_op jit(solution)/shard_map/ppermute | solution.py:34
  137.2 6.4 %collective-permute-start.14 = (bf16[512,256]{1,0:T(8,128)(2,1)S(1)}, bf16[512,256]{1,0:T(8,128)(2,1)S(1)}, u32[]{:S(2)}, u32[]{:S(2)}) collective-permute-start(bf16[512,256]{1,0:T(8,128)(2,1)S(1)} %slice.156), channel_id=1, source_target_pairs={{0,4},{1,5},{2,6},{3,7},{4,12},{5,13},{6,14},{7,15},{8,0},{9,1},{1... | collective-permute-start | bytes 786440 | tf_op jit(solution)/shard_map/ppermute | solution.py:34
  145.1 9.9 %collective-permute-start.15 = (f32[256,1024]{1,0:T(8,128)S(1)}, f32[256,1024]{1,0:T(8,128)S(1)}, u32[]{:S(2)}, u32[]{:S(2)}) collective-permute-start(f32[256,1024]{1,0:T(8,128)S(1)} %get-tuple-element.72), channel_id=1, source_target_pairs={{0,1},{1,0},{2,3},{3,2},{4,5},{5,4},{6,7},{7,6},{8,9},{9,8},{10,11... | collective-permute-start | bytes 3145736 | tf_op jit(solution)/shard_map/ppermute | solution.py:37
  148.0 25.3 %collective-permute-start.17 = (f32[256,1024]{1,0:T(8,128)S(1)}, f32[256,1024]{1,0:T(8,128)S(1)}, u32[]{:S(2)}, u32[]{:S(2)}) collective-permute-start(f32[256,1024]{1,0:T(8,128)S(1)} %slice_add_fusion), channel_id=1, source_target_pairs={{0,2},{1,3},{2,0},{3,1},{4,6},{5,7},{6,4},{7,5},{8,10},{9,11},{10,... | collective-permute-start | bytes 3145736 | tf_op jit(solution)/shard_map/ppermute | solution.py:37
  153.1 26.4 %collective-permute-start.23 = (f32[2,1024]{1,0:T(2,128)S(1)}, f32[2,1024]{1,0:T(2,128)S(1)}, u32[]{:S(2)}, u32[]{:S(2)}) collective-permute-start(f32[2,1024]{1,0:T(2,128)S(1)} %pad_maximum_fusion.8), channel_id=1, source_target_pairs={{0,8},{1,9},{2,10},{3,11},{4,12},{5,13},{6,14},{7,15},{8,0},{9,1},... | collective-permute-start | bytes 24584 | tf_op jit(solution)/shard_map/ppermute | solution.py:34
  173.5 22.2 %collective-permute-start.25 = (bf16[256,1024]{1,0:T(8,128)(2,1)S(1)}, bf16[256,1024]{1,0:T(8,128)(2,1)S(1)}, u32[]{:S(2)}, u32[]{:S(2)}) collective-permute-start(bf16[256,1024]{1,0:T(8,128)(2,1)S(1)} %get-tuple-element.42.refs_0_), channel_id=1, source_target_pairs={{8,0},{9,1},{10,2},{11,3},{12,4},{13,5},{14,6},{15,7},{16,8},{17,9... | collective-permute-start | bytes 1572872 | tf_op jit(solution)/shard_map/ppermute | solution.py:34
  174.8 22.2 %collective-permute-start.28 = (bf16[256,1024]{1,0:T(8,128)(2,1)S(1)}, bf16[256,1024]{1,0:T(8,128)(2,1)S(1)}, u32[]{:S(2)}, u32[]{:S(2)}) collective-permute-start(bf16[256,1024]{1,0:T(8,128)(2,1)S(1)} %get-tuple-element.42.refs_0_), channel_id=1, source_target_pairs={{0,8},{1,9},{2,10},{3,11},{4,12},{5,13},{6,14},{7,15},{8,16},{9,17... | collective-permute-start | bytes 1572872 | tf_op jit(solution)/shard_map/ppermute | solution.py:34
  179.5 13.7 %collective-permute-start.24 = (f32[4,1024]{1,0:T(4,128)S(1)}, f32[4,1024]{1,0:T(4,128)S(1)}, u32[]{:S(2)}, u32[]{:S(2)}) collective-permute-start(f32[4,1024]{1,0:T(4,128)S(1)} %pad_maximum_fusion.3), channel_id=1, source_target_pairs={{0,16},{1,17},{2,18},{3,19},{4,20},{5,21},{6,22},{7,23},{8,24},{9,... | collective-permute-start | bytes 49160 | tf_op jit(solution)/shard_map/ppermute | solution.py:34
  182.9 7.3 %collective-permute-start.18 = (f32[256]{0:T(256)S(1)}, f32[256]{0:T(256)S(1)}, u32[]{:S(2)}, u32[]{:S(2)}) collective-permute-start(f32[256]{0:T(256)S(1)} %get-tuple-element.70), channel_id=1, source_target_pairs={{0,8},{1,9},{2,10},{3,11},{4,12},{5,13},{6,14},{7,15},{8,0},{9,1},... | collective-permute-start | bytes 3080 | tf_op jit(solution)/shard_map/ppermute | solution.py:34
  182.9 18.0 %collective-permute-start.32 = (bf16[256,1024]{1,0:T(8,128)(2,1)S(1)}, bf16[256,1024]{1,0:T(8,128)(2,1)S(1)}, u32[]{:S(2)}, u32[]{:S(2)}) collective-permute-start(bf16[256,1024]{1,0:T(8,128)(2,1)S(1)} %get-tuple-element.42.refs_0_), channel_id=1, source_target_pairs={{0,4},{1,5},{2,6},{3,7},{4,0},{5,1},{6,2},{7,3},{8,12},{9,13},{10,... | collective-permute-start | bytes 1572872 | tf_op jit(solution)/shard_map/ppermute | solution.py:34
  190.2 4.6 %collective-permute-start.19 = (f32[256]{0:T(256)S(1)}, f32[256]{0:T(256)S(1)}, u32[]{:S(2)}, u32[]{:S(2)}) collective-permute-start(f32[256]{0:T(256)S(1)} %add.139), channel_id=1, source_target_pairs={{0,16},{1,17},{2,18},{3,19},{4,20},{5,21},{6,22},{7,23},{8,24},{9,... | collective-permute-start | bytes 3080 | tf_op jit(solution)/shard_map/ppermute | solution.py:34
  194.8 5.3 %collective-permute-start.20 = (f32[256]{0:T(256)S(1)}, f32[256]{0:T(256)S(1)}, u32[]{:S(2)}, u32[]{:S(2)}) collective-permute-start(f32[256]{0:T(256)S(1)} %add.140), channel_id=1, source_target_pairs={{0,4},{1,5},{2,6},{3,7},{4,0},{5,1},{6,2},{7,3},{8,12},{9,13},{10,... | collective-permute-start | bytes 3080 | tf_op jit(solution)/shard_map/ppermute | solution.py:34
  195.8 13.3 %collective-permute-start.26 = (bf16[256,1024]{1,0:T(8,128)(2,1)S(1)}, bf16[256,1024]{1,0:T(8,128)(2,1)S(1)}, u32[]{:S(2)}, u32[]{:S(2)}) collective-permute-start(bf16[256,1024]{1,0:T(8,128)(2,1)S(1)} %collective-permute-done.25), channel_id=1, source_target_pairs={{8,0},{9,1},{10,2},{11,3},{12,4},{13,5},{14,6},{15,7},{16,8},{17,9... | collective-permute-start | bytes 1572872 | tf_op jit(solution)/shard_map/ppermute | solution.py:34
  197.1 12.0 %collective-permute-start.29 = (bf16[256,1024]{1,0:T(8,128)(2,1)S(1)}, bf16[256,1024]{1,0:T(8,128)(2,1)}, u32[]{:S(2)}, u32[]{:S(2)}) collective-permute-start(bf16[256,1024]{1,0:T(8,128)(2,1)S(1)} %collective-permute-done.28), channel_id=1, source_target_pairs={{8,16},{9,17},{10,18},{11,19},{12,20},{13,21},{14,22},{15,23},{16,... | collective-permute-start | bytes 1572872 | tf_op jit(solution)/shard_map/ppermute | solution.py:34
  198.6 14.9 %collective-permute-start.31 = (bf16[256,1024]{1,0:T(8,128)(2,1)S(1)}, bf16[256,1024]{1,0:T(8,128)(2,1)S(1)}, u32[]{:S(2)}, u32[]{:S(2)}) collective-permute-start(bf16[256,1024]{1,0:T(8,128)(2,1)S(1)} %get-tuple-element.42.refs_0_), channel_id=1, source_target_pairs={{0,2},{1,3},{2,0},{3,1},{4,6},{5,7},{6,4},{7,5},{8,10},{9,11},{10,... | collective-permute-start | bytes 1572872 | tf_op jit(solution)/shard_map/ppermute | solution.py:37
  200.3 23.1 %collective-permute-start.21 = (f32[256,1]{1,0:T(8,128)S(1)}, f32[256,1]{1,0:T(8,128)S(1)}, u32[]{:S(2)}, u32[]{:S(2)}) collective-permute-start(f32[256,1]{1,0:T(8,128)S(1)} %copy.23.scale_ref), channel_id=1, source_target_pairs={{0,2},{1,3},{2,0},{3,1},{4,6},{5,7},{6,4},{7,5},{8,10},{9,11},{10,... | collective-permute-start | bytes 3080 | tf_op jit(solution)/shard_map/ppermute | solution.py:37
  200.9 22.5 %collective-permute-start.33 = (bf16[256,1024]{1,0:T(8,128)(2,1)S(1)}, bf16[256,1024]{1,0:T(8,128)(2,1)S(1)}, u32[]{:S(2)}, u32[]{:S(2)}) collective-permute-start(bf16[256,1024]{1,0:T(8,128)(2,1)S(1)} %collective-permute-done.32.refs_2_), channel_id=1, source_target_pairs={{0,2},{1,3},{2,0},{3,1},{4,6},{5,7},{6,4},{7,5},{8,10},{9,11},{10,... | collective-permute-start | bytes 1572872 | tf_op jit(solution)/shard_map/ppermute | solution.py:37
  223.9 15.4 %collective-permute-start.34 = (bf16[2,512,1024]{2,1,0:T(8,128)(2,1)S(1)}, bf16[2,512,1024]{2,1,0:T(8,128)(2,1)S(1)}, u32[]{:S(2)}, u32[]{:S(2)}) collective-permute-start(bf16[2,512,1024]{2,1,0:T(8,128)(2,1)S(1)} %shard_map.153.own_ref), channel_id=1, source_target_pairs={{0,1},{1,0},{2,3},{3,2},{4,5},{5,4},{6,7},{7,6},{8,9},{9,8},{10,11... | collective-permute-start | bytes 6291464 | tf_op jit(solution)/shard_map/ppermute | solution.py:37
  224.0 14.3 %collective-permute-start.42 = (bf16[256,1024]{1,0:T(8,128)(2,1)S(1)}, bf16[256,1024]{1,0:T(8,128)(2,1)S(1)}, u32[]{:S(2)}, u32[]{:S(2)}) collective-permute-start(bf16[256,1024]{1,0:T(8,128)(2,1)S(1)} %broadcast_select_fusion.refs_0_), channel_id=1, source_target_pairs={{0,2},{1,3},{2,0},{3,1},{4,6},{5,7},{6,4},{7,5},{8,10},{9,11},{10,... | collective-permute-start | bytes 1572872 | tf_op jit(solution)/shard_map/ppermute | solution.py:37
  225.6 26.6 %collective-permute-start.43 = (bf16[256,1024]{1,0:T(8,128)(2,1)S(1)}, bf16[256,1024]{1,0:T(8,128)(2,1)S(1)}, u32[]{:S(2)}, u32[]{:S(2)}) collective-permute-start(bf16[256,1024]{1,0:T(8,128)(2,1)S(1)} %broadcast_select_fusion.refs_0_), channel_id=1, source_target_pairs={{0,4},{1,5},{2,6},{3,7},{4,0},{5,1},{6,2},{7,3},{8,12},{9,13},{10,... | collective-permute-start | bytes 1572872 | tf_op jit(solution)/shard_map/ppermute | solution.py:34
  226.6 36.7 %collective-permute-start.39 = (bf16[256,1024]{1,0:T(8,128)(2,1)S(1)}, bf16[256,1024]{1,0:T(8,128)(2,1)S(1)}, u32[]{:S(2)}, u32[]{:S(2)}) collective-permute-start(bf16[256,1024]{1,0:T(8,128)(2,1)S(1)} %select_select_fusion.1.refs_0_), channel_id=1, source_target_pairs={{0,4},{1,5},{2,6},{3,7},{4,0},{5,1},{6,2},{7,3},{8,12},{9,13},{10,... | collective-permute-start | bytes 1572872 | tf_op jit(solution)/shard_map/ppermute | solution.py:34
  238.3 23.7 %collective-permute-start.44 = (bf16[256,1024]{1,0:T(8,128)(2,1)S(1)}, bf16[256,1024]{1,0:T(8,128)(2,1)S(1)}, u32[]{:S(2)}, u32[]{:S(2)}) collective-permute-start(bf16[256,1024]{1,0:T(8,128)(2,1)S(1)} %collective-permute-done.42.refs_1_), channel_id=1, source_target_pairs={{0,4},{1,5},{2,6},{3,7},{4,0},{5,1},{6,2},{7,3},{8,12},{9,13},{10,... | collective-permute-start | bytes 1572872 | tf_op jit(solution)/shard_map/ppermute | solution.py:34
  262.6 41.8 %collective-permute-start.45 = (bf16[2,512,1024]{2,1,0:T(8,128)(2,1)S(1)}, bf16[2,512,1024]{2,1,0:T(8,128)(2,1)S(1)}, u32[]{:S(2)}, u32[]{:S(2)}) collective-permute-start(bf16[2,512,1024]{2,1,0:T(8,128)(2,1)S(1)} %shard_map.156.own_ref), channel_id=1, source_target_pairs={{0,1},{1,0},{2,3},{3,2},{4,5},{5,4},{6,7},{7,6},{8,9},{9,8},{10,11... | collective-permute-start | bytes 6291464 | tf_op jit(solution)/shard_map/ppermute | solution.py:37
  262.7 14.9 %collective-permute-start.38 = (bf16[256,1024]{1,0:T(8,128)(2,1)S(1)}, bf16[256,1024]{1,0:T(8,128)(2,1)S(1)}, u32[]{:S(2)}, u32[]{:S(2)}) collective-permute-start(bf16[256,1024]{1,0:T(8,128)(2,1)S(1)} %select_select_fusion.1.refs_0_), channel_id=1, source_target_pairs={{0,2},{1,3},{2,0},{3,1},{4,6},{5,7},{6,4},{7,5},{8,10},{9,11},{10,... | collective-permute-start | bytes 1572872 | tf_op jit(solution)/shard_map/ppermute | solution.py:37
  263.3 25.0 %collective-permute-start.40 = (bf16[256,1024]{1,0:T(8,128)(2,1)S(1)}, bf16[256,1024]{1,0:T(8,128)(2,1)S(1)}, u32[]{:S(2)}, u32[]{:S(2)}) collective-permute-start(bf16[256,1024]{1,0:T(8,128)(2,1)S(1)} %collective-permute-done.39.refs_2_), channel_id=1, source_target_pairs={{0,2},{1,3},{2,0},{3,1},{4,6},{5,7},{6,4},{7,5},{8,10},{9,11},{10,... | collective-permute-start | bytes 1572872 | tf_op jit(solution)/shard_map/ppermute | solution.py:37
  264.8 24.1 %collective-permute-start.27 = (bf16[256,1024]{1,0:T(8,128)(2,1)S(1)}, bf16[256,1024]{1,0:T(8,128)(2,1)S(1)}, u32[]{:S(2)}, u32[]{:S(2)}) collective-permute-start(bf16[256,1024]{1,0:T(8,128)(2,1)S(1)} %collective-permute-done.26), channel_id=1, source_target_pairs={{8,0},{9,1},{10,2},{11,3},{12,4},{13,5},{14,6},{15,7}} | collective-permute-start | bytes 1572872 | tf_op jit(solution)/shard_map/ppermute | solution.py:34
  266.1 22.8 %collective-permute-start.30 = (bf16[256,1024]{1,0:T(8,128)(2,1)}, bf16[256,1024]{1,0:T(8,128)(2,1)S(1)}, u32[]{:S(2)}, u32[]{:S(2)}) collective-permute-start(bf16[256,1024]{1,0:T(8,128)(2,1)} %collective-permute-done.29), channel_id=1, source_target_pairs={{16,24},{17,25},{18,26},{19,27},{20,28},{21,29},{22,30},{23,31}} | collective-permute-start | bytes 1572872 | tf_op jit(solution)/shard_map/ppermute | solution.py:34
  288.8 30.0 %collective-permute-start.41 = (bf16[2,512,1024]{2,1,0:T(8,128)(2,1)S(1)}, bf16[2,512,1024]{2,1,0:T(8,128)(2,1)S(1)}, u32[]{:S(2)}, u32[]{:S(2)}) collective-permute-start(bf16[2,512,1024]{2,1,0:T(8,128)(2,1)S(1)} %shard_map.155.own_ref), channel_id=1, source_target_pairs={{0,1},{1,0},{2,3},{3,2},{4,5},{5,4},{6,7},{7,6},{8,9},{9,8},{10,11... | collective-permute-start | bytes 6291464 | tf_op jit(solution)/shard_map/ppermute | solution.py:37
  289.1 14.4 %collective-permute-start.35 = (bf16[256,1024]{1,0:T(8,128)(2,1)S(1)}, bf16[256,1024]{1,0:T(8,128)(2,1)S(1)}, u32[]{:S(2)}, u32[]{:S(2)}) collective-permute-start(bf16[256,1024]{1,0:T(8,128)(2,1)S(1)} %select_select_fusion.refs_0_), channel_id=1, source_target_pairs={{0,2},{1,3},{2,0},{3,1},{4,6},{5,7},{6,4},{7,5},{8,10},{9,11},{10,... | collective-permute-start | bytes 1572872 | tf_op jit(solution)/shard_map/ppermute | solution.py:37
  289.6 43.6 %collective-permute-start.36 = (bf16[256,1024]{1,0:T(8,128)(2,1)S(1)}, bf16[256,1024]{1,0:T(8,128)(2,1)S(1)}, u32[]{:S(2)}, u32[]{:S(2)}) collective-permute-start(bf16[256,1024]{1,0:T(8,128)(2,1)S(1)} %select_select_fusion.refs_0_), channel_id=1, source_target_pairs={{0,4},{1,5},{2,6},{3,7},{4,0},{5,1},{6,2},{7,3},{8,12},{9,13},{10,... | collective-permute-start | bytes 1572872 | tf_op jit(solution)/shard_map/ppermute | solution.py:34
  303.4 29.8 %collective-permute-start.37 = (bf16[256,1024]{1,0:T(8,128)(2,1)S(1)}, bf16[256,1024]{1,0:T(8,128)(2,1)S(1)}, u32[]{:S(2)}, u32[]{:S(2)}) collective-permute-start(bf16[256,1024]{1,0:T(8,128)(2,1)S(1)} %collective-permute-done.35.refs_1_), channel_id=1, source_target_pairs={{0,4},{1,5},{2,6},{3,7},{4,0},{5,1},{6,2},{7,3},{8,12},{9,13},{10,... | collective-permute-start | bytes 1572872 | tf_op jit(solution)/shard_map/ppermute | solution.py:34
  333.8 4.4 %collective-permute-start.46 = (bf16[2,512,1024]{2,1,0:T(8,128)(2,1)S(1)}, bf16[2,512,1024]{2,1,0:T(8,128)(2,1)}, u32[]{:S(2)}, u32[]{:S(2)}) collective-permute-start(bf16[2,512,1024]{2,1,0:T(8,128)(2,1)S(1)} %shard_map.159.own_ref), channel_id=1, source_target_pairs={{0,1},{1,0},{2,3},{3,2},{4,5},{5,4},{6,7},{7,6},{8,9},{9,8},{10,11... | collective-permute-start | bytes 6291464 | tf_op jit(solution)/shard_map/ppermute | solution.py:37
  368.4 7.6 %collective-permute-start.50 = (f32[3,1024]{1,0:T(4,128)S(1)}, f32[3,1024]{1,0:T(4,128)S(1)}, u32[]{:S(2)}, u32[]{:S(2)}) collective-permute-start(f32[3,1024]{1,0:T(4,128)S(1)} %pad_maximum_fusion.6), channel_id=1, source_target_pairs={{0,8},{1,9},{2,10},{3,11},{4,12},{5,13},{6,14},{7,15},{8,0},{9,1},... | collective-permute-start | bytes 36872 | tf_op jit(solution)/shard_map/ppermute | solution.py:34
  376.0 4.7 %collective-permute-start.51 = (f32[3,1024]{1,0:T(4,128)S(1)}, f32[3,1024]{1,0:T(4,128)S(1)}, u32[]{:S(2)}, u32[]{:S(2)}) collective-permute-start(f32[3,1024]{1,0:T(4,128)S(1)} %pad_maximum_fusion.7), channel_id=1, source_target_pairs={{0,16},{1,17},{2,18},{3,19},{4,20},{5,21},{6,22},{7,23},{8,24},{9,... | collective-permute-start | bytes 36872 | tf_op jit(solution)/shard_map/ppermute | solution.py:34
  (14 other events, 236.1 us)
